TPU v7x, 256 devices: a whole 4x4x8 slice. The times are simulated.
256 devices in a mesh: dp: 16 (over x_hi, y, core), hid: 16 (over x_lo, z).
Axes of the slice: x: 4 (x_hi: 2, x_lo: 2; x = x_hi * 2 + x_lo), y: 4, z: 8, core: 2. Of those that a mesh axis runs over, the one named last changes fastest.
Arguments:
- tokens: bfloat16 [2048, 4096], P('dp', 'hid'), may hold values from -6 to 6
- expert_ids: int32 [2048, 2], P('dp'), may hold values from 0 to 7, all different within a row; in each aligned block of 128 rows (0 to 127, 128 to 255, ...) at most 48 rows name the same one
- gate_levels: int32 [2048, 2], P('dp'), may hold values from 1 to 255
- w_gate: bfloat16 [4096, 114688], P(None, ('dp', 'hid')), may hold values from -0.09375 to 0.09375
- w_up: bfloat16 [4096, 114688], P(None, ('dp', 'hid')), may hold values from -0.09375 to 0.09375
- w_down: bfloat16 [114688, 4096], P(('dp', 'hid')), may hold values from -0.046875 to 0.046875
Outputs:
- mixed: bfloat16 [2048, 4096], P('dp', 'hid')
Inputs may be any that keep to these rules, and one draw needn't show every extreme that they name: `expert_ids`: each row names two different experts. Among the 128 rows of one index of dp no expert is named by more than 48 rows, and in some such block one expert is named by exactly 48 rows.
All inputs are finite; a program needn't handle non-finite values.
Results may differ from a plain program's by a relative error of at most 0.019.
Values may be sent and summed in bfloat16 or wider, within the bound.
A program may use at most 64 MiB of HBM per device.

v0:
```python
import jax
import jax.numpy as jnp
from jax import lax
from jax.sharding import PartitionSpec as P

EXPERTS = 8


def hid_rings(n_hid):
    n_z = n_hid // 2
    swap = [(h, h ^ n_z) for h in range(n_hid)]
    cw = [(h, (h // n_z) * n_z + (h % n_z + 1) % n_z) for h in range(n_hid)]
    ccw = [(h, (h // n_z) * n_z + (h % n_z - 1) % n_z) for h in range(n_hid)]
    return n_z, swap, cw, ccw


def gather_hid(x):
    n_hid = lax.axis_size("hid")
    n_z, swap, cw, ccw = hid_rings(n_hid)
    h = lax.axis_index("hid")
    z, x_lo = h % n_z, h // n_z
    y = lax.ppermute(x, "hid", swap)
    pair = jnp.where(x_lo == 0, jnp.stack([x, y], 1), jnp.stack([y, x], 1))
    rel = [pair] * n_z
    a = b = pair
    for s in range(1, n_z // 2 + 1):
        a = lax.ppermute(a, "hid", cw)
        rel[s] = a
        if s < n_z - s:
            b = lax.ppermute(b, "hid", ccw)
            rel[n_z - s] = b
    rel = jnp.stack(rel, 0)
    order = (z - jnp.arange(n_z)) % n_z
    full = jnp.take(rel, order, axis=0)
    rows, chunk = x.shape
    return full.transpose(1, 2, 0, 3).reshape(rows, n_hid * chunk)


def scatter_hid(p):
    n_hid = lax.axis_size("hid")
    n_z, swap, cw, ccw = hid_rings(n_hid)
    h = lax.axis_index("hid")
    z, x_lo = h % n_z, h // n_z
    rows = p.shape[0]
    chunk = p.shape[1] // n_hid
    half = rows // 2
    pt = p.reshape(rows, 2, n_z, chunk).transpose(2, 0, 1, 3)
    top, bottom = pt[:, :half], pt[:, half:]
    a = jnp.take(top, (z - 1) % n_z, axis=0)
    b = jnp.take(bottom, (z + 1) % n_z, axis=0)
    for s in range(n_z - 1):
        ra = lax.ppermute(a.astype(jnp.bfloat16), "hid", cw)
        rb = lax.ppermute(b.astype(jnp.bfloat16), "hid", ccw)
        a = ra.astype(jnp.float32) + jnp.take(top, (z - s - 2) % n_z, axis=0).astype(jnp.float32)
        b = rb.astype(jnp.float32) + jnp.take(bottom, (z + s + 2) % n_z, axis=0).astype(jnp.float32)
    block = jnp.concatenate([a, b], 0)
    give = jnp.where(x_lo == 0, block[:, 1], block[:, 0])
    keep = jnp.where(x_lo == 0, block[:, 0], block[:, 1])
    got = lax.ppermute(give.astype(jnp.bfloat16), "hid", swap)
    return (keep + got.astype(jnp.float32)).astype(jnp.bfloat16)


def local(tokens, expert_ids, gate_levels, w_gate, w_up, w_down):
    devices_dp = lax.axis_size("dp")
    halves_each = devices_dp // EXPERTS
    tok_rows = expert_ids.shape[0]
    capacity = 3 * tok_rows // 8
    part_cap = capacity // halves_each
    chunk = tokens.shape[1]
    flat_ids = expert_ids.reshape(-1)
    total = flat_ids.shape[0]
    one_hot = (flat_ids[:, None] == jnp.arange(EXPERTS, dtype=jnp.int32)[None, :]).astype(jnp.int32)
    earlier = jnp.cumsum(one_hot, axis=0) - one_hot
    slot_of = jnp.sum(earlier * one_hot, axis=1)
    dest_row = flat_ids * capacity + slot_of
    src_token = (
        jnp.full((EXPERTS * capacity,), -1, jnp.int32)
        .at[dest_row]
        .set(jnp.arange(total, dtype=jnp.int32) // 2)
    )
    filled = src_token >= 0
    src_index = jnp.maximum(src_token, 0)
    levels = gate_levels.astype(jnp.float32)
    gate_frac = levels / jnp.sum(levels, axis=1, keepdims=True)

    picked = jnp.where(filled[:, None], tokens[src_index], jnp.zeros((), tokens.dtype))
    picked = picked.reshape(devices_dp, part_cap, chunk)
    received = lax.all_to_all(picked, "dp", split_axis=0, concat_axis=0, tiled=True)
    rows_mine = received.reshape(devices_dp * part_cap, chunk)
    x_mine = gather_hid(rows_mine)

    pairs = [(i, i ^ 1) for i in range(devices_dp)]
    w_down_partner = lax.ppermute(w_down, "dp", pairs)
    x_other = lax.ppermute(x_mine, "dp", pairs)

    def hidden_of(x):
        gate = jnp.dot(x, w_gate, preferred_element_type=jnp.float32)
        up = jnp.dot(x, w_up, preferred_element_type=jnp.float32)
        return (jax.nn.silu(gate) * up).astype(jnp.bfloat16)

    h_mine = hidden_of(x_mine)
    h_other = hidden_of(x_other)
    h_back = lax.ppermute(h_other, "dp", pairs)
    both = jnp.dot(h_mine, w_down, preferred_element_type=jnp.float32) + jnp.dot(
        h_back, w_down_partner, preferred_element_type=jnp.float32
    )
    summed = scatter_hid(both.astype(jnp.bfloat16))
    returned = lax.all_to_all(
        summed.reshape(devices_dp, part_cap, chunk), "dp", split_axis=0, concat_axis=0, tiled=True
    )
    back = returned.reshape(EXPERTS * capacity, chunk).astype(jnp.float32)
    chosen = back[dest_row] * gate_frac.reshape(-1)[:, None]
    return chosen.reshape(tok_rows, 2, chunk).sum(axis=1).astype(jnp.bfloat16)


def solution(mesh):
    placed = (
        P("dp", "hid"),
        P("dp", None),
        P("dp", None),
        P(None, ("dp", "hid")),
        P(None, ("dp", "hid")),
        P(("dp", "hid"), None),
    )
    return jax.shard_map(
        local, mesh=mesh, in_specs=placed, out_specs=P("dp", "hid"), check_vma=False
    )
```

profile of v0, /device:TPU:1, one launch (start us, length us, event | category | flops | bytes accessed | tf_op | source)
XLA Modules:
  0.0 196.6 jit_solution(5532511142889920613)
XLA Ops:
  7.3 16.4 %all_to_all.10 = bf16[16,24,256]{2,1,0:T(8,128)(2,1)S(1)} all-to-all(bf16[16,24,256]{2,1,0:T(8,128)(2,1)S(1)} %broadcast_select_fusion), channel_id=1, replica_groups=mesh['dp'=16,'hid'=16] {'dp'}, dimensions={0} | all-to-all | bytes 393216 | tf_op jit(solution)/shard_map/all_to_all | solution.py:88
  24.0 5.4 %collective-permute-done = bf16[384,256]{1,0:T(8,128)(2,1)S(1)} collective-permute-done((bf16[384,256]{1,0:T(8,128)(2,1)S(1)}, bf16[384,256]{1,0:T(8,128)(2,1)S(1)}, u32[]{:S(2)}, u32[]{:S(2)}) %collective-permute-start) | collective-permute-done | bytes 196640 | tf_op jit(solution)/shard_map/ppermute | solution.py:22
  31.1 4.0 %collective-permute-start.5 = (bf16[384,2,256]{2,0,1:T(8,128)(2,1)S(1)}, bf16[384,2,256]{2,0,1:T(8,128)(2,1)S(1)}, u32[]{:S(2)}, u32[]{:S(2)}) collective-permute-start(bf16[384,2,256]{2,0,1:T(8,128)(2,1)S(1)} %maximum_select_fusion.1), channel_id=1, source_target_pairs={{0,7},{1,0},{2,1},{3,2},{4,3},{5,4},{6,5},{7,6},{8,15},{9,8},{10,9... | collective-permute-start | bytes 1179656 | tf_op jit(solution)/shard_map/ppermute | solution.py:30
  35.1 7.8 %collective-permute-done.1 = bf16[384,2,256]{2,0,1:T(8,128)(2,1)S(1)} collective-permute-done((bf16[384,2,256]{2,0,1:T(8,128)(2,1)S(1)}, bf16[384,2,256]{2,0,1:T(8,128)(2,1)S(1)}, u32[]{:S(2)}, u32[]{:S(2)}) %collective-permute-start.1) | collective-permute-done | bytes 393248 | tf_op jit(solution)/shard_map/ppermute | solution.py:27
  42.9 2.7 %collective-permute-start.6 = (bf16[384,2,256]{2,0,1:T(8,128)(2,1)S(1)}, bf16[384,2,256]{2,0,1:T(8,128)(2,1)S(1)}, u32[]{:S(2)}, u32[]{:S(2)}) collective-permute-start(bf16[384,2,256]{2,0,1:T(8,128)(2,1)S(1)} %collective-permute-done.5), channel_id=1, source_target_pairs={{0,7},{1,0},{2,1},{3,2},{4,3},{5,4},{6,5},{7,6},{8,15},{9,8},{10,9... | collective-permute-start | bytes 1179656 | tf_op jit(solution)/shard_map/ppermute | solution.py:30
  45.7 6.9 %collective-permute-done.2 = bf16[384,2,256]{2,0,1:T(8,128)(2,1)S(1)} collective-permute-done((bf16[384,2,256]{2,0,1:T(8,128)(2,1)S(1)}, bf16[384,2,256]{2,0,1:T(8,128)(2,1)S(1)}, u32[]{:S(2)}, u32[]{:S(2)}) %collective-permute-start.2) | collective-permute-done | bytes 393248 | tf_op jit(solution)/shard_map/ppermute | solution.py:27
  54.2 2.7 %collective-permute-start.7 = (bf16[384,2,256]{2,0,1:T(8,128)(2,1)S(1)}, bf16[384,2,256]{2,0,1:T(8,128)(2,1)S(1)}, u32[]{:S(2)}, u32[]{:S(2)}) collective-permute-start(bf16[384,2,256]{2,0,1:T(8,128)(2,1)S(1)} %collective-permute-done.6), channel_id=1, source_target_pairs={{0,7},{1,0},{2,1},{3,2},{4,3},{5,4},{6,5},{7,6},{8,15},{9,8},{10,9... | collective-permute-start | bytes 1179656 | tf_op jit(solution)/shard_map/ppermute | solution.py:30
  56.8 4.5 %collective-permute-done.3 = bf16[384,2,256]{2,0,1:T(8,128)(2,1)S(1)} collective-permute-done((bf16[384,2,256]{2,0,1:T(8,128)(2,1)S(1)}, bf16[384,2,256]{2,0,1:T(8,128)(2,1)S(1)}, u32[]{:S(2)}, u32[]{:S(2)}) %collective-permute-start.3) | collective-permute-done | bytes 393248 | tf_op jit(solution)/shard_map/ppermute | solution.py:27
  62.9 6.3 %collective-permute-done.4 = bf16[384,2,256]{2,0,1:T(8,128)(2,1)S(1)} collective-permute-done((bf16[384,2,256]{2,0,1:T(8,128)(2,1)S(1)}, bf16[384,2,256]{2,0,1:T(8,128)(2,1)S(1)}, u32[]{:S(2)}, u32[]{:S(2)}) %collective-permute-start.4) | collective-permute-done | bytes 393248 | tf_op jit(solution)/shard_map/ppermute | solution.py:27
  77.0 3.4 %copy.28 = bf16[384,2,8,256]{0,3,2,1:T(8,128)(2,1)S(1)} copy(bf16[384,2,8,256]{3,0,1,2:T(8,128)(2,1)} %select_bitcast_fusion) | data formatting | bytes 6291456 | tf_op jit(solution)/shard_map/jit(_take)/select_n | solution.py:34
  80.4 5.2 %collective-permute-start.8 = (bf16[384,4096]{0,1:T(8,128)(2,1)S(1)}, bf16[384,4096]{0,1:T(8,128)(2,1)}, u32[]{:S(2)}, u32[]{:S(2)}) collective-permute-start(bf16[384,4096]{0,1:T(8,128)(2,1)S(1)} %bitcast.97), channel_id=1, source_target_pairs={{0,16},{16,0},{32,48},{48,32},{64,80},{80,64},{96,112},{112,96},{1... | collective-permute-start | bytes 9437192 | tf_op jit(solution)/shard_map/ppermute | solution.py:94
  85.9 5.1 %fusion.22 = f32[384,448]{0,1:T(8,128)} fusion(bf16[4096,448]{0,1:T(8,128)(2,1)} %param.11, bf16[384,4096]{0,1:T(8,128)(2,1)S(1)} %bitcast.98), kind=kOutput, calls=%fused_computation.90 | convolution fusion | flops 1409286144 | bytes 7503872 | tf_op jit(solution)/shard_map/dot_general | solution.py:97
  91.0 4.1 %fusion.23 = f32[384,448]{0,1:T(8,128)S(1)} fusion(bf16[4096,448]{0,1:T(8,128)(2,1)S(1)} %copy-done.4, bf16[384,4096]{0,1:T(8,128)(2,1)} %collective-permute-done.8), kind=kOutput, calls=%fused_computation.91 | convolution fusion | flops 1409286144 | bytes 7503872 | tf_op jit(solution)/shard_map/dot_general | solution.py:97
  95.1 4.7 %multiply_convert_fusion = bf16[384,448]{0,1:T(8,128)(2,1)} fusion(f32[384,448]{0,1:T(8,128)S(1)} %fusion.23, bf16[4096,448]{0,1:T(8,128)(2,1)S(1)} %copy-done.5, bf16[384,4096]{0,1:T(8,128)(2,1)} %collective-permute-done.8), kind=kOutput, calls=%fused_computation.12 | convolution fusion | flops 1410318336 | bytes 7847936 | tf_op jit(solution)/shard_map/dot_general | solution.py:98
  100.2 9.9 %fusion.1 = f32[384,4096]{1,0:T(8,128)} fusion(bf16[448,4096]{1,0:T(8,128)(2,1)} %param.13, bf16[4096,448]{0,1:T(8,128)(2,1)} %param.12, bf16[384,4096]{0,1:T(8,128)(2,1)S(1)} %bitcast.99, f32[384,448]{0,1:T(8,128)} %fusion.22), kind=kOutput, calls=%fused_computation.9 | convolution fusion | flops 2819604480 | bytes 17465344 | tf_op jit(solution)/shard_map/dot_general | solution.py:104
  110.1 5.7 %add_convert_fusion = bf16[384,4096]{1,0:T(8,128)(2,1)S(1)} fusion(f32[384,4096]{1,0:T(8,128)} %fusion.1, bf16[384,448]{0,1:T(8,128)(2,1)S(1)} %collective-permute-done.9, bf16[448,4096]{1,0:T(8,128)(2,1)} %collective-permute-done.10), kind=kOutput, calls=%fused_computation.4 | convolution fusion | flops 1412431872 | bytes 13451264 | tf_op jit(solution)/shard_map/dot_general | solution.py:104
  121.4 4.9 %collective-permute-done.11 = bf16[192,2,256]{2,0,1:T(8,128)(2,1)} collective-permute-done((bf16[192,2,256]{2,0,1:T(8,128)(2,1)S(1)}, bf16[192,2,256]{2,0,1:T(8,128)(2,1)}, u32[]{:S(2)}, u32[]{:S(2)}) %collective-permute-start.11) | collective-permute-done | bytes 196640 | tf_op jit(solution)/shard_map/ppermute | solution.py:52
  127.4 2.7 %collective-permute-start.19 = (bf16[192,2,256]{2,0,1:T(8,128)(2,1)S(1)}, bf16[192,2,256]{2,0,1:T(8,128)(2,1)S(1)}, u32[]{:S(2)}, u32[]{:S(2)}) collective-permute-start(bf16[192,2,256]{2,0,1:T(8,128)(2,1)S(1)} %add_convert_fusion.6), channel_id=1, source_target_pairs={{0,7},{1,0},{2,1},{3,2},{4,3},{5,4},{6,5},{7,6},{8,15},{9,8},{10,9... | collective-permute-start | bytes 589832 | tf_op jit(solution)/shard_map/ppermute | solution.py:53
  130.1 3.9 %collective-permute-done.12 = bf16[192,2,256]{2,0,1:T(8,128)(2,1)S(1)} collective-permute-done((bf16[192,2,256]{2,0,1:T(8,128)(2,1)S(1)}, bf16[192,2,256]{2,0,1:T(8,128)(2,1)S(1)}, u32[]{:S(2)}, u32[]{:S(2)}) %collective-permute-start.12) | collective-permute-done | bytes 196640 | tf_op jit(solution)/shard_map/ppermute | solution.py:52
  134.2 2.7 %collective-permute-start.20 = (bf16[192,2,256]{2,0,1:T(8,128)(2,1)S(1)}, bf16[192,2,256]{2,0,1:T(8,128)(2,1)S(1)}, u32[]{:S(2)}, u32[]{:S(2)}) collective-permute-start(bf16[192,2,256]{2,0,1:T(8,128)(2,1)S(1)} %add_convert_fusion.5), channel_id=1, source_target_pairs={{0,7},{1,0},{2,1},{3,2},{4,3},{5,4},{6,5},{7,6},{8,15},{9,8},{10,9... | collective-permute-start | bytes 589832 | tf_op jit(solution)/shard_map/ppermute | solution.py:53
  137.0 2.9 %collective-permute-done.13 = bf16[192,2,256]{2,0,1:T(8,128)(2,1)S(1)} collective-permute-done((bf16[192,2,256]{2,0,1:T(8,128)(2,1)S(1)}, bf16[192,2,256]{2,0,1:T(8,128)(2,1)S(1)}, u32[]{:S(2)}, u32[]{:S(2)}) %collective-permute-start.13) | collective-permute-done | bytes 196640 | tf_op jit(solution)/shard_map/ppermute | solution.py:52
  140.1 2.7 %collective-permute-start.21 = (bf16[192,2,256]{2,0,1:T(8,128)(2,1)S(1)}, bf16[192,2,256]{2,0,1:T(8,128)(2,1)S(1)}, u32[]{:S(2)}, u32[]{:S(2)}) collective-permute-start(bf16[192,2,256]{2,0,1:T(8,128)(2,1)S(1)} %add_convert_fusion.4), channel_id=1, source_target_pairs={{0,7},{1,0},{2,1},{3,2},{4,3},{5,4},{6,5},{7,6},{8,15},{9,8},{10,9... | collective-permute-start | bytes 589832 | tf_op jit(solution)/shard_map/ppermute | solution.py:53
  142.9 2.9 %collective-permute-done.14 = bf16[192,2,256]{2,0,1:T(8,128)(2,1)S(1)} collective-permute-done((bf16[192,2,256]{2,0,1:T(8,128)(2,1)S(1)}, bf16[192,2,256]{2,0,1:T(8,128)(2,1)S(1)}, u32[]{:S(2)}, u32[]{:S(2)}) %collective-permute-start.14) | collective-permute-done | bytes 196640 | tf_op jit(solution)/shard_map/ppermute | solution.py:52
  146.0 2.7 %collective-permute-start.22 = (bf16[192,2,256]{2,0,1:T(8,128)(2,1)S(1)}, bf16[192,2,256]{2,0,1:T(8,128)(2,1)S(1)}, u32[]{:S(2)}, u32[]{:S(2)}) collective-permute-start(bf16[192,2,256]{2,0,1:T(8,128)(2,1)S(1)} %add_convert_fusion.3), channel_id=1, source_target_pairs={{0,7},{1,0},{2,1},{3,2},{4,3},{5,4},{6,5},{7,6},{8,15},{9,8},{10,9... | collective-permute-start | bytes 589832 | tf_op jit(solution)/shard_map/ppermute | solution.py:53
  148.7 2.9 %collective-permute-done.15 = bf16[192,2,256]{2,0,1:T(8,128)(2,1)S(1)} collective-permute-done((bf16[192,2,256]{2,0,1:T(8,128)(2,1)S(1)}, bf16[192,2,256]{2,0,1:T(8,128)(2,1)S(1)}, u32[]{:S(2)}, u32[]{:S(2)}) %collective-permute-start.15) | collective-permute-done | bytes 196640 | tf_op jit(solution)/shard_map/ppermute | solution.py:52
  151.9 2.7 %collective-permute-start.23 = (bf16[192,2,256]{2,0,1:T(8,128)(2,1)S(1)}, bf16[192,2,256]{2,0,1:T(8,128)(2,1)S(1)}, u32[]{:S(2)}, u32[]{:S(2)}) collective-permute-start(bf16[192,2,256]{2,0,1:T(8,128)(2,1)S(1)} %add_convert_fusion.2), channel_id=1, source_target_pairs={{0,7},{1,0},{2,1},{3,2},{4,3},{5,4},{6,5},{7,6},{8,15},{9,8},{10,9... | collective-permute-start | bytes 589832 | tf_op jit(solution)/shard_map/ppermute | solution.py:53
  154.6 3.7 %collective-permute-done.16 = bf16[192,2,256]{2,0,1:T(8,128)(2,1)S(1)} collective-permute-done((bf16[192,2,256]{2,0,1:T(8,128)(2,1)S(1)}, bf16[192,2,256]{2,0,1:T(8,128)(2,1)S(1)}, u32[]{:S(2)}, u32[]{:S(2)}) %collective-permute-start.16) | collective-permute-done | bytes 196640 | tf_op jit(solution)/shard_map/ppermute | solution.py:52
  158.6 3.0 %collective-permute-start.24 = (bf16[192,2,256]{2,0,1:T(8,128)(2,1)S(1)}, bf16[192,2,256]{2,0,1:T(8,128)(2,1)S(1)}, u32[]{:S(2)}, u32[]{:S(2)}) collective-permute-start(bf16[192,2,256]{2,0,1:T(8,128)(2,1)S(1)} %add_convert_fusion.1), channel_id=1, source_target_pairs={{0,7},{1,0},{2,1},{3,2},{4,3},{5,4},{6,5},{7,6},{8,15},{9,8},{10,9... | collective-permute-start | bytes 589832 | tf_op jit(solution)/shard_map/ppermute | solution.py:53
  161.6 4.8 %collective-permute-done.17 = bf16[192,2,256]{2,0,1:T(8,128)(2,1)S(1)} collective-permute-done((bf16[192,2,256]{2,0,1:T(8,128)(2,1)S(1)}, bf16[192,2,256]{2,0,1:T(8,128)(2,1)S(1)}, u32[]{:S(2)}, u32[]{:S(2)}) %collective-permute-start.17) | collective-permute-done | bytes 196640 | tf_op jit(solution)/shard_map/ppermute | solution.py:52
  167.0 4.5 %collective-permute-done.25 = bf16[384,256]{1,0:T(8,128)(2,1)S(1)} collective-permute-done((bf16[384,256]{1,0:T(8,128)(2,1)S(1)}, bf16[384,256]{1,0:T(8,128)(2,1)S(1)}, u32[]{:S(2)}, u32[]{:S(2)}) %collective-permute-start.25) | collective-permute-done | bytes 196640 | tf_op jit(solution)/shard_map/ppermute | solution.py:59
  172.2 14.0 %all-to-all-start.1 = ((bf16[16,24,256]{2,1,0:T(8,128)(2,1)}), bf16[16,24,256]{2,1,0:T(8,128)(2,1)S(1)}, u32[]{:S(2)}, u32[]{:S(2)}) async-start(bf16[16,24,256]{2,1,0:T(8,128)(2,1)} %bitcast.39), calls=%async_computation.1 | async-start | bytes 393216 | tf_op jit(solution)/shard_map/all_to_all | solution.py:108
  186.4 8.0 %all-to-all-done.1 = bf16[16,24,256]{2,1,0:T(8,128)(2,1)S(1)} async-done(((bf16[16,24,256]{2,1,0:T(8,128)(2,1)}), bf16[16,24,256]{2,1,0:T(8,128)(2,1)S(1)}, u32[]{:S(2)}, u32[]{:S(2)}) %all-to-all-start.1) | async-done | bytes 196640 | tf_op jit(solution)/shard_map/all_to_all | solution.py:108
  (105 shorter events, 32.0 us)
Async XLA Ops:
  0.0 5.1 %copy-start = (bf16[128,256]{1,0:T(8,128)(2,1)S(1)}, bf16[128,256]{1,0:T(8,128)(2,1)}, u32[]{:S(2)}) copy-start(bf16[128,256]{1,0:T(8,128)(2,1)} %param.8) | copy-start | bytes 196612
  23.7 5.7 %collective-permute-start = (bf16[384,256]{1,0:T(8,128)(2,1)S(1)}, bf16[384,256]{1,0:T(8,128)(2,1)S(1)}, u32[]{:S(2)}, u32[]{:S(2)}) collective-permute-start(bf16[384,256]{1,0:T(8,128)(2,1)S(1)} %bitcast.100), channel_id=1, source_target_pairs={{0,8},{1,9},{2,10},{3,11},{4,12},{5,13},{6,14},{7,15},{8,0},{9,1},... | collective-permute-start | bytes 589832 | tf_op jit(solution)/shard_map/ppermute | solution.py:22
  29.4 13.5 %collective-permute-start.1 = (bf16[384,2,256]{2,0,1:T(8,128)(2,1)S(1)}, bf16[384,2,256]{2,0,1:T(8,128)(2,1)S(1)}, u32[]{:S(2)}, u32[]{:S(2)}) collective-permute-start(bf16[384,2,256]{2,0,1:T(8,128)(2,1)S(1)} %maximum_select_fusion.1), channel_id=1, source_target_pairs={{0,1},{1,2},{2,3},{3,4},{4,5},{5,6},{6,7},{7,0},{8,9},{9,10},{10,1... | collective-permute-start | bytes 1179656 | tf_op jit(solution)/shard_map/ppermute | solution.py:27
  31.1 11.8 %collective-permute-start.5 = (bf16[384,2,256]{2,0,1:T(8,128)(2,1)S(1)}, bf16[384,2,256]{2,0,1:T(8,128)(2,1)S(1)}, u32[]{:S(2)}, u32[]{:S(2)}) collective-permute-start(bf16[384,2,256]{2,0,1:T(8,128)(2,1)S(1)} %maximum_select_fusion.1), channel_id=1, source_target_pairs={{0,7},{1,0},{2,1},{3,2},{4,3},{5,4},{6,5},{7,6},{8,15},{9,8},{10,9... | collective-permute-start | bytes 1179656 | tf_op jit(solution)/shard_map/ppermute | solution.py:30
  42.9 9.7 %collective-permute-start.2 = (bf16[384,2,256]{2,0,1:T(8,128)(2,1)S(1)}, bf16[384,2,256]{2,0,1:T(8,128)(2,1)S(1)}, u32[]{:S(2)}, u32[]{:S(2)}) collective-permute-start(bf16[384,2,256]{2,0,1:T(8,128)(2,1)S(1)} %collective-permute-done.1), channel_id=1, source_target_pairs={{0,1},{1,2},{2,3},{3,4},{4,5},{5,6},{6,7},{7,0},{8,9},{9,10},{10,1... | collective-permute-start | bytes 1179656 | tf_op jit(solution)/shard_map/ppermute | solution.py:27
  42.9 11.2 %collective-permute-start.6 = (bf16[384,2,256]{2,0,1:T(8,128)(2,1)S(1)}, bf16[384,2,256]{2,0,1:T(8,128)(2,1)S(1)}, u32[]{:S(2)}, u32[]{:S(2)}) collective-permute-start(bf16[384,2,256]{2,0,1:T(8,128)(2,1)S(1)} %collective-permute-done.5), channel_id=1, source_target_pairs={{0,7},{1,0},{2,1},{3,2},{4,3},{5,4},{6,5},{7,6},{8,15},{9,8},{10,9... | collective-permute-start | bytes 1179656 | tf_op jit(solution)/shard_map/ppermute | solution.py:30
  52.6 8.8 %collective-permute-start.3 = (bf16[384,2,256]{2,0,1:T(8,128)(2,1)S(1)}, bf16[384,2,256]{2,0,1:T(8,128)(2,1)S(1)}, u32[]{:S(2)}, u32[]{:S(2)}) collective-permute-start(bf16[384,2,256]{2,0,1:T(8,128)(2,1)S(1)} %collective-permute-done.2), channel_id=1, source_target_pairs={{0,1},{1,2},{2,3},{3,4},{4,5},{5,6},{6,7},{7,0},{8,9},{9,10},{10,1... | collective-permute-start | bytes 1179656 | tf_op jit(solution)/shard_map/ppermute | solution.py:27
  54.2 15.8 %collective-permute-start.7 = (bf16[384,2,256]{2,0,1:T(8,128)(2,1)S(1)}, bf16[384,2,256]{2,0,1:T(8,128)(2,1)S(1)}, u32[]{:S(2)}, u32[]{:S(2)}) collective-permute-start(bf16[384,2,256]{2,0,1:T(8,128)(2,1)S(1)} %collective-permute-done.6), channel_id=1, source_target_pairs={{0,7},{1,0},{2,1},{3,2},{4,3},{5,4},{6,5},{7,6},{8,15},{9,8},{10,9... | collective-permute-start | bytes 1179656 | tf_op jit(solution)/shard_map/ppermute | solution.py:30
  61.4 7.8 %collective-permute-start.4 = (bf16[384,2,256]{2,0,1:T(8,128)(2,1)S(1)}, bf16[384,2,256]{2,0,1:T(8,128)(2,1)S(1)}, u32[]{:S(2)}, u32[]{:S(2)}) collective-permute-start(bf16[384,2,256]{2,0,1:T(8,128)(2,1)S(1)} %collective-permute-done.3), channel_id=1, source_target_pairs={{0,1},{1,2},{2,3},{3,4},{4,5},{5,6},{6,7},{7,0},{8,9},{9,10},{10,1... | collective-permute-start | bytes 1179656 | tf_op jit(solution)/shard_map/ppermute | solution.py:27
  80.4 10.6 %collective-permute-start.8 = (bf16[384,4096]{0,1:T(8,128)(2,1)S(1)}, bf16[384,4096]{0,1:T(8,128)(2,1)}, u32[]{:S(2)}, u32[]{:S(2)}) collective-permute-start(bf16[384,4096]{0,1:T(8,128)(2,1)S(1)} %bitcast.97), channel_id=1, source_target_pairs={{0,16},{16,0},{32,48},{48,32},{64,80},{80,64},{96,112},{112,96},{1... | collective-permute-start | bytes 9437192 | tf_op jit(solution)/shard_map/ppermute | solution.py:94
  85.6 24.5 %collective-permute-start.10 = (bf16[448,4096]{1,0:T(8,128)(2,1)}, bf16[448,4096]{1,0:T(8,128)(2,1)}, u32[]{:S(2)}, u32[]{:S(2)}) collective-permute-start(bf16[448,4096]{1,0:T(8,128)(2,1)} %param.13), channel_id=1, source_target_pairs={{0,16},{16,0},{32,48},{48,32},{64,80},{80,64},{96,112},{112,96},{1... | collective-permute-start | bytes 11010056 | tf_op jit(solution)/shard_map/ppermute | solution.py:93
  85.9 5.1 %copy-start.4 = (bf16[4096,448]{0,1:T(8,128)(2,1)S(1)}, bf16[4096,448]{0,1:T(8,128)(2,1)}, u32[]{:S(2)}) copy-start(bf16[4096,448]{0,1:T(8,128)(2,1)} %param.11) | copy-start | bytes 11010052
  91.0 4.1 %copy-start.5 = (bf16[4096,448]{0,1:T(8,128)(2,1)S(1)}, bf16[4096,448]{0,1:T(8,128)(2,1)}, u32[]{:S(2)}) copy-start(bf16[4096,448]{0,1:T(8,128)(2,1)} %param.12) | copy-start | bytes 11010052
  99.9 10.2 %collective-permute-start.9 = (bf16[384,448]{0,1:T(8,128)(2,1)}, bf16[384,448]{0,1:T(8,128)(2,1)S(1)}, u32[]{:S(2)}, u32[]{:S(2)}) collective-permute-start(bf16[384,448]{0,1:T(8,128)(2,1)} %multiply_convert_fusion), channel_id=1, source_target_pairs={{0,16},{16,0},{32,48},{48,32},{64,80},{80,64},{96,112},{112,96},{1... | collective-permute-start | bytes 1032200 | tf_op jit(solution)/shard_map/ppermute | solution.py:103
  118.3 7.9 %collective-permute-start.11 = (bf16[192,2,256]{2,0,1:T(8,128)(2,1)S(1)}, bf16[192,2,256]{2,0,1:T(8,128)(2,1)}, u32[]{:S(2)}, u32[]{:S(2)}) collective-permute-start(bf16[192,2,256]{2,0,1:T(8,128)(2,1)S(1)} %select_bitcast_fusion.2), channel_id=1, source_target_pairs={{0,1},{1,2},{2,3},{3,4},{4,5},{5,6},{6,7},{7,0},{8,9},{9,10},{10,1... | collective-permute-start | bytes 589832 | tf_op jit(solution)/shard_map/ppermute | solution.py:52
  119.0 8.3 %collective-permute-start.18 = (bf16[192,2,256]{2,0,1:T(8,128)(2,1)S(1)}, bf16[192,2,256]{2,0,1:T(8,128)(2,1)S(1)}, u32[]{:S(2)}, u32[]{:S(2)}) collective-permute-start(bf16[192,2,256]{2,0,1:T(8,128)(2,1)S(1)} %select_bitcast_fusion.1), channel_id=1, source_target_pairs={{0,7},{1,0},{2,1},{3,2},{4,3},{5,4},{6,5},{7,6},{8,15},{9,8},{10,9... | collective-permute-start | bytes 589832 | tf_op jit(solution)/shard_map/ppermute | solution.py:53
  127.2 6.8 %collective-permute-start.12 = (bf16[192,2,256]{2,0,1:T(8,128)(2,1)S(1)}, bf16[192,2,256]{2,0,1:T(8,128)(2,1)S(1)}, u32[]{:S(2)}, u32[]{:S(2)}) collective-permute-start(bf16[192,2,256]{2,0,1:T(8,128)(2,1)S(1)} %add_convert_fusion.12), channel_id=1, source_target_pairs={{0,1},{1,2},{2,3},{3,4},{4,5},{5,6},{6,7},{7,0},{8,9},{9,10},{10,1... | collective-permute-start | bytes 589832 | tf_op jit(solution)/shard_map/ppermute | solution.py:52
  127.4 6.7 %collective-permute-start.19 = (bf16[192,2,256]{2,0,1:T(8,128)(2,1)S(1)}, bf16[192,2,256]{2,0,1:T(8,128)(2,1)S(1)}, u32[]{:S(2)}, u32[]{:S(2)}) collective-permute-start(bf16[192,2,256]{2,0,1:T(8,128)(2,1)S(1)} %add_convert_fusion.6), channel_id=1, source_target_pairs={{0,7},{1,0},{2,1},{3,2},{4,3},{5,4},{6,5},{7,6},{8,15},{9,8},{10,9... | collective-permute-start | bytes 589832 | tf_op jit(solution)/shard_map/ppermute | solution.py:53
  134.1 5.8 %collective-permute-start.13 = (bf16[192,2,256]{2,0,1:T(8,128)(2,1)S(1)}, bf16[192,2,256]{2,0,1:T(8,128)(2,1)S(1)}, u32[]{:S(2)}, u32[]{:S(2)}) collective-permute-start(bf16[192,2,256]{2,0,1:T(8,128)(2,1)S(1)} %add_convert_fusion.11), channel_id=1, source_target_pairs={{0,1},{1,2},{2,3},{3,4},{4,5},{5,6},{6,7},{7,0},{8,9},{9,10},{10,1... | collective-permute-start | bytes 589832 | tf_op jit(solution)/shard_map/ppermute | solution.py:52
  134.2 5.8 %collective-permute-start.20 = (bf16[192,2,256]{2,0,1:T(8,128)(2,1)S(1)}, bf16[192,2,256]{2,0,1:T(8,128)(2,1)S(1)}, u32[]{:S(2)}, u32[]{:S(2)}) collective-permute-start(bf16[192,2,256]{2,0,1:T(8,128)(2,1)S(1)} %add_convert_fusion.5), channel_id=1, source_target_pairs={{0,7},{1,0},{2,1},{3,2},{4,3},{5,4},{6,5},{7,6},{8,15},{9,8},{10,9... | collective-permute-start | bytes 589832 | tf_op jit(solution)/shard_map/ppermute | solution.py:53
  139.9 5.8 %collective-permute-start.14 = (bf16[192,2,256]{2,0,1:T(8,128)(2,1)S(1)}, bf16[192,2,256]{2,0,1:T(8,128)(2,1)S(1)}, u32[]{:S(2)}, u32[]{:S(2)}) collective-permute-start(bf16[192,2,256]{2,0,1:T(8,128)(2,1)S(1)} %add_convert_fusion.10), channel_id=1, source_target_pairs={{0,1},{1,2},{2,3},{3,4},{4,5},{5,6},{6,7},{7,0},{8,9},{9,10},{10,1... | collective-permute-start | bytes 589832 | tf_op jit(solution)/shard_map/ppermute | solution.py:52
  140.1 26.9 %copy-start.3 = (s32[128,2]{0,1:T(2,128)S(1)}, s32[128,2]{0,1:T(2,128)}, u32[]{:S(2)}) copy-start(s32[128,2]{0,1:T(2,128)} %param.10) | copy-start | bytes 3076
  140.1 5.8 %collective-permute-start.21 = (bf16[192,2,256]{2,0,1:T(8,128)(2,1)S(1)}, bf16[192,2,256]{2,0,1:T(8,128)(2,1)S(1)}, u32[]{:S(2)}, u32[]{:S(2)}) collective-permute-start(bf16[192,2,256]{2,0,1:T(8,128)(2,1)S(1)} %add_convert_fusion.4), channel_id=1, source_target_pairs={{0,7},{1,0},{2,1},{3,2},{4,3},{5,4},{6,5},{7,6},{8,15},{9,8},{10,9... | collective-permute-start | bytes 589832 | tf_op jit(solution)/shard_map/ppermute | solution.py:53
  145.8 5.8 %collective-permute-start.15 = (bf16[192,2,256]{2,0,1:T(8,128)(2,1)S(1)}, bf16[192,2,256]{2,0,1:T(8,128)(2,1)S(1)}, u32[]{:S(2)}, u32[]{:S(2)}) collective-permute-start(bf16[192,2,256]{2,0,1:T(8,128)(2,1)S(1)} %add_convert_fusion.9), channel_id=1, source_target_pairs={{0,1},{1,2},{2,3},{3,4},{4,5},{5,6},{6,7},{7,0},{8,9},{9,10},{10,1... | collective-permute-start | bytes 589832 | tf_op jit(solution)/shard_map/ppermute | solution.py:52
  146.0 40.4 %copy-start.2 = (s32[256,1]{0,1:T(1,128)S(1)}, s32[256,1]{0,1:T(1,128)}, u32[]{:S(2)}) copy-start(s32[256,1]{0,1:T(1,128)} %copy-done.1) | copy-start | bytes 3076
  146.0 5.8 %collective-permute-start.22 = (bf16[192,2,256]{2,0,1:T(8,128)(2,1)S(1)}, bf16[192,2,256]{2,0,1:T(8,128)(2,1)S(1)}, u32[]{:S(2)}, u32[]{:S(2)}) collective-permute-start(bf16[192,2,256]{2,0,1:T(8,128)(2,1)S(1)} %add_convert_fusion.3), channel_id=1, source_target_pairs={{0,7},{1,0},{2,1},{3,2},{4,3},{5,4},{6,5},{7,6},{8,15},{9,8},{10,9... | collective-permute-start | bytes 589832 | tf_op jit(solution)/shard_map/ppermute | solution.py:53
  151.7 6.6 %collective-permute-start.16 = (bf16[192,2,256]{2,0,1:T(8,128)(2,1)S(1)}, bf16[192,2,256]{2,0,1:T(8,128)(2,1)S(1)}, u32[]{:S(2)}, u32[]{:S(2)}) collective-permute-start(bf16[192,2,256]{2,0,1:T(8,128)(2,1)S(1)} %add_convert_fusion.8), channel_id=1, source_target_pairs={{0,1},{1,2},{2,3},{3,4},{4,5},{5,6},{6,7},{7,0},{8,9},{9,10},{10,1... | collective-permute-start | bytes 589832 | tf_op jit(solution)/shard_map/ppermute | solution.py:52
  151.9 6.6 %collective-permute-start.23 = (bf16[192,2,256]{2,0,1:T(8,128)(2,1)S(1)}, bf16[192,2,256]{2,0,1:T(8,128)(2,1)S(1)}, u32[]{:S(2)}, u32[]{:S(2)}) collective-permute-start(bf16[192,2,256]{2,0,1:T(8,128)(2,1)S(1)} %add_convert_fusion.2), channel_id=1, source_target_pairs={{0,7},{1,0},{2,1},{3,2},{4,3},{5,4},{6,5},{7,6},{8,15},{9,8},{10,9... | collective-permute-start | bytes 589832 | tf_op jit(solution)/shard_map/ppermute | solution.py:53
  158.4 8.0 %collective-permute-start.17 = (bf16[192,2,256]{2,0,1:T(8,128)(2,1)S(1)}, bf16[192,2,256]{2,0,1:T(8,128)(2,1)S(1)}, u32[]{:S(2)}, u32[]{:S(2)}) collective-permute-start(bf16[192,2,256]{2,0,1:T(8,128)(2,1)S(1)} %add_convert_fusion.7), channel_id=1, source_target_pairs={{0,1},{1,2},{2,3},{3,4},{4,5},{5,6},{6,7},{7,0},{8,9},{9,10},{10,1... | collective-permute-start | bytes 589832 | tf_op jit(solution)/shard_map/ppermute | solution.py:52
  158.6 7.8 %collective-permute-start.24 = (bf16[192,2,256]{2,0,1:T(8,128)(2,1)S(1)}, bf16[192,2,256]{2,0,1:T(8,128)(2,1)S(1)}, u32[]{:S(2)}, u32[]{:S(2)}) collective-permute-start(bf16[192,2,256]{2,0,1:T(8,128)(2,1)S(1)} %add_convert_fusion.1), channel_id=1, source_target_pairs={{0,7},{1,0},{2,1},{3,2},{4,3},{5,4},{6,5},{7,6},{8,15},{9,8},{10,9... | collective-permute-start | bytes 589832 | tf_op jit(solution)/shard_map/ppermute | solution.py:53
  166.6 4.9 %collective-permute-start.25 = (bf16[384,256]{1,0:T(8,128)(2,1)S(1)}, bf16[384,256]{1,0:T(8,128)(2,1)S(1)}, u32[]{:S(2)}, u32[]{:S(2)}) collective-permute-start(bf16[384,256]{1,0:T(8,128)(2,1)S(1)} %fusion.11), channel_id=1, source_target_pairs={{0,8},{1,9},{2,10},{3,11},{4,12},{5,13},{6,14},{7,15},{8,0},{9,1},... | collective-permute-start | bytes 589832 | tf_op jit(solution)/shard_map/ppermute | solution.py:59
  172.2 22.2 %all-to-all-start.1 = ((bf16[16,24,256]{2,1,0:T(8,128)(2,1)}), bf16[16,24,256]{2,1,0:T(8,128)(2,1)S(1)}, u32[]{:S(2)}, u32[]{:S(2)}) async-start(bf16[16,24,256]{2,1,0:T(8,128)(2,1)} %bitcast.39), calls=%async_computation.1 | async-start | bytes 393216 | tf_op jit(solution)/shard_map/all_to_all | solution.py:108
  (1 other events, 0.6 us)
where the time goes:
time: 197 us
  waiting for transfers between devices  69.2 us (35%)
  starting transfers between devices  51.6 us (26%)
  matrix products  29.5 us (15%)
  local copies, waits for them, and re-layouts  20.9 us (11%)
  blocking collectives  16.4 us (8%)
  other arithmetic  8.26 us (4%)
    ppermute x7, waiting for transfers between devices, scatter_hid(): ra = lax.ppermute(a.astype(jnp.bfloat16), 'hid', cw)  25.9 us
    ppermute x4, waiting for transfers between devices, gather_hid(): a = lax.ppermute(a, 'hid', cw)  25.4 us
    ppermute x7, starting transfers between devices, scatter_hid(): rb = lax.ppermute(b.astype(jnp.bfloat16), 'hid', ccw)  19 us
    all_to_all x1, blocking collectives, local(): lax.all_to_all(picked, 'dp', split_axis=0, concat_axis=0, tiled=True)  16.4 us
    all_to_all x1, starting transfers between devices, local(): lax.all_to_all(summed.reshape(devices_dp, part_cap, chunk), 'dp', split_a...  14 us
    dot_general x1, matrix products, local(): jnp.dot(h_mine, w_down, preferred_element_type=jnp.float32)  9.86 us
    ppermute x3, starting transfers between devices, gather_hid(): b = lax.ppermute(b, 'hid', ccw)  9.45 us
    dot_general x2, matrix products, hidden_of(): gate = jnp.dot(x, w_gate, preferred_element_type=jnp.float32)  9.22 us
  transfers between devices with their start and end apart: 27, of which 14 were waited for; matrix products, arithmetic and copies ran while one was open for 15% of the time, Pallas kernels for 0%

commit v1 on v0

--- a/solution.py
+++ b/solution.py
@@ -48,11 +48,15 @@
     top, bottom = pt[:, :half], pt[:, half:]
     a = jnp.take(top, (z - 1) % n_z, axis=0)
     b = jnp.take(bottom, (z + 1) % n_z, axis=0)
-    for s in range(n_z - 1):
+    def step(s, carry):
+        a, b = carry
         ra = lax.ppermute(a.astype(jnp.bfloat16), "hid", cw)
         rb = lax.ppermute(b.astype(jnp.bfloat16), "hid", ccw)
-        a = ra.astype(jnp.float32) + jnp.take(top, (z - s - 2) % n_z, axis=0).astype(jnp.float32)
-        b = rb.astype(jnp.float32) + jnp.take(bottom, (z + s + 2) % n_z, axis=0).astype(jnp.float32)
+        a = ra.astype(jnp.float32) + lax.dynamic_index_in_dim(top, (z - s - 2) % n_z, 0, False).astype(jnp.float32)
+        b = rb.astype(jnp.float32) + lax.dynamic_index_in_dim(bottom, (z + s + 2) % n_z, 0, False).astype(jnp.float32)
+        return a, b
+
+    a, b = lax.fori_loop(0, n_z - 1, step, (a.astype(jnp.float32), b.astype(jnp.float32)))
     block = jnp.concatenate([a, b], 0)
     give = jnp.where(x_lo == 0, block[:, 1], block[:, 0])
     keep = jnp.where(x_lo == 0, block[:, 0], block[:, 1])

time: 197 us -> 211 us (1.071)
  other arithmetic: 8.26 us -> 18 us
  starting transfers between devices: 51.6 us -> 43.7 us
  waiting for transfers between devices: 69.2 us -> 77 us
  local copies, waits for them, and re-layouts: 20.9 us -> 25 us
    add x2 -> x14, other arithmetic: 0.12 us -> 9.35 us  [the longest x7 7.91 us: step(): ra.astype(jnp.float32)]
    ppermute x14, starting transfers between devices: 19.8 us -> 11.3 us  [the longest x7 9.25 us: step(): ra = lax.ppermute(a.astype(jnp.bfloat16), 'hid', cw)]
    ppermute x14, waiting for transfers between devices: 25.9 us -> 33.8 us  [the longest x7 23.4 us: step(): rb = lax.ppermute(b.astype(jnp.bfloat16), 'hid', ccw)]
    unnamed x20 -> x23, local copies, waits for them, and re-layouts: 7.08 us -> 7.97 us
  transfers between devices with their start and end apart: 27 -> 27, of which waited for: 14 -> 21; matrix products, arithmetic and copies ran while one was open for 15% -> 14% of each run, Pallas kernels for 0% -> 0%
where the time goes in v1:
time: 211 us; the launch traced here: 210 us
  waiting for transfers between devices  77 us (36%)
  starting transfers between devices  43.7 us (21%)
  matrix products  29.6 us (14%)
  local copies, waits for them, and re-layouts  25 us (12%)
  other arithmetic  18 us (9%)
  blocking collectives  16.4 us (8%)
    ppermute x4, waiting for transfers between devices, gather_hid(): a = lax.ppermute(a, 'hid', cw)  25.4 us
    ppermute x7, waiting for transfers between devices, step(): rb = lax.ppermute(b.astype(jnp.bfloat16), 'hid', ccw)  23.4 us
    all_to_all x1, blocking collectives, local(): lax.all_to_all(picked, 'dp', split_axis=0, concat_axis=0, tiled=True)  16.4 us
    all_to_all x1, starting transfers between devices, local(): lax.all_to_all(summed.reshape(devices_dp, part_cap, chunk), 'dp', split_a...  14.7 us
    ppermute x7, waiting for transfers between devices, step(): ra = lax.ppermute(a.astype(jnp.bfloat16), 'hid', cw)  10.3 us
    dot_general x1, matrix products, local(): jnp.dot(h_mine, w_down, preferred_element_type=jnp.float32)  9.86 us
    ppermute x3, starting transfers between devices, gather_hid(): b = lax.ppermute(b, 'hid', ccw)  9.45 us
    ppermute x7, starting transfers between devices, step(): ra = lax.ppermute(a.astype(jnp.bfloat16), 'hid', cw)  9.25 us
  transfers between devices with their start and end apart: 27, of which 21 were waited for; matrix products, arithmetic and copies ran while one was open for 14% of the time, Pallas kernels for 0%

profile of v1, /device:TPU:1, one launch (start us, length us, event | category | flops | bytes accessed | tf_op | source)
XLA Modules:
  0.0 210.2 jit_solution(15636461534029142179)
XLA Ops:
  5.1 2.1 gather_fusion
  7.3 16.4 %all_to_all.10 = bf16[16,24,256]{2,1,0:T(8,128)(2,1)S(1)} all-to-all(bf16[16,24,256]{2,1,0:T(8,128)(2,1)S(1)} %broadcast_select_fusion.2), channel_id=1, replica_groups=mesh['dp'=16,'hid'=16] {'dp'}, dimensions={0} | all-to-all | bytes 393216 | tf_op jit(solution)/shard_map/all_to_all | solution.py:92
  24.0 5.4 %collective-permute-done.2 = bf16[384,256]{1,0:T(8,128)(2,1)S(1)} collective-permute-done((bf16[384,256]{1,0:T(8,128)(2,1)S(1)}, bf16[384,256]{1,0:T(8,128)(2,1)S(1)}, u32[]{:S(2)}, u32[]{:S(2)}) %collective-permute-start.2) | collective-permute-done | bytes 196640 | tf_op jit(solution)/shard_map/ppermute | solution.py:22
  31.1 4.0 %collective-permute-start.7 = (bf16[384,2,256]{2,0,1:T(8,128)(2,1)S(1)}, bf16[384,2,256]{2,0,1:T(8,128)(2,1)S(1)}, u32[]{:S(2)}, u32[]{:S(2)}) collective-permute-start(bf16[384,2,256]{2,0,1:T(8,128)(2,1)S(1)} %maximum_select_fusion.1), channel_id=1, source_target_pairs={{0,7},{1,0},{2,1},{3,2},{4,3},{5,4},{6,5},{7,6},{8,15},{9,8},{10,9... | collective-permute-start | bytes 1179656 | tf_op jit(solution)/shard_map/ppermute | solution.py:30
  35.1 7.8 %collective-permute-done.3 = bf16[384,2,256]{2,0,1:T(8,128)(2,1)S(1)} collective-permute-done((bf16[384,2,256]{2,0,1:T(8,128)(2,1)S(1)}, bf16[384,2,256]{2,0,1:T(8,128)(2,1)S(1)}, u32[]{:S(2)}, u32[]{:S(2)}) %collective-permute-start.3) | collective-permute-done | bytes 393248 | tf_op jit(solution)/shard_map/ppermute | solution.py:27
  42.9 2.7 %collective-permute-start.8 = (bf16[384,2,256]{2,0,1:T(8,128)(2,1)S(1)}, bf16[384,2,256]{2,0,1:T(8,128)(2,1)S(1)}, u32[]{:S(2)}, u32[]{:S(2)}) collective-permute-start(bf16[384,2,256]{2,0,1:T(8,128)(2,1)S(1)} %collective-permute-done.7), channel_id=1, source_target_pairs={{0,7},{1,0},{2,1},{3,2},{4,3},{5,4},{6,5},{7,6},{8,15},{9,8},{10,9... | collective-permute-start | bytes 1179656 | tf_op jit(solution)/shard_map/ppermute | solution.py:30
  45.7 6.9 %collective-permute-done.4 = bf16[384,2,256]{2,0,1:T(8,128)(2,1)S(1)} collective-permute-done((bf16[384,2,256]{2,0,1:T(8,128)(2,1)S(1)}, bf16[384,2,256]{2,0,1:T(8,128)(2,1)S(1)}, u32[]{:S(2)}, u32[]{:S(2)}) %collective-permute-start.4) | collective-permute-done | bytes 393248 | tf_op jit(solution)/shard_map/ppermute | solution.py:27
  54.2 2.7 %collective-permute-start.9 = (bf16[384,2,256]{2,0,1:T(8,128)(2,1)S(1)}, bf16[384,2,256]{2,0,1:T(8,128)(2,1)S(1)}, u32[]{:S(2)}, u32[]{:S(2)}) collective-permute-start(bf16[384,2,256]{2,0,1:T(8,128)(2,1)S(1)} %collective-permute-done.8), channel_id=1, source_target_pairs={{0,7},{1,0},{2,1},{3,2},{4,3},{5,4},{6,5},{7,6},{8,15},{9,8},{10,9... | collective-permute-start | bytes 1179656 | tf_op jit(solution)/shard_map/ppermute | solution.py:30
  56.9 4.5 %collective-permute-done.5 = bf16[384,2,256]{2,0,1:T(8,128)(2,1)S(1)} collective-permute-done((bf16[384,2,256]{2,0,1:T(8,128)(2,1)S(1)}, bf16[384,2,256]{2,0,1:T(8,128)(2,1)S(1)}, u32[]{:S(2)}, u32[]{:S(2)}) %collective-permute-start.5) | collective-permute-done | bytes 393248 | tf_op jit(solution)/shard_map/ppermute | solution.py:27
  62.9 6.3 %collective-permute-done.6 = bf16[384,2,256]{2,0,1:T(8,128)(2,1)S(1)} collective-permute-done((bf16[384,2,256]{2,0,1:T(8,128)(2,1)S(1)}, bf16[384,2,256]{2,0,1:T(8,128)(2,1)S(1)}, u32[]{:S(2)}, u32[]{:S(2)}) %collective-permute-start.6) | collective-permute-done | bytes 393248 | tf_op jit(solution)/shard_map/ppermute | solution.py:27
  72.4 2.6 %gather_fusion.1 = bf16[8,384,2,256]{3,1,2,0:T(8,128)(2,1)S(1)} fusion(bf16[8,384,2,256]{3,1,2,0:T(8,128)(2,1)} %bitcast_dynamic-update-slice_fusion, s32[1024]{0:T(1024)S(1)} %pad_clamp_fusion.1), kind=kCustom, calls=%fused_computation.1 | custom fusion | bytes 6291488 | tf_op jit(solution)/shard_map/jit(_take)/gather | solution.py:34
  75.0 2.0 select_bitcast_fusion
  77.0 3.4 %copy.23 = bf16[384,2,8,256]{0,3,2,1:T(8,128)(2,1)S(1)} copy(bf16[384,2,8,256]{3,0,1,2:T(8,128)(2,1)} %select_bitcast_fusion) | data formatting | bytes 6291456 | tf_op jit(solution)/shard_map/jit(_take)/select_n | solution.py:34
  80.5 5.2 %collective-permute-start.10 = (bf16[384,4096]{0,1:T(8,128)(2,1)S(1)}, bf16[384,4096]{0,1:T(8,128)(2,1)}, u32[]{:S(2)}, u32[]{:S(2)}) collective-permute-start(bf16[384,4096]{0,1:T(8,128)(2,1)S(1)} %bitcast.83), channel_id=1, source_target_pairs={{0,16},{16,0},{32,48},{48,32},{64,80},{80,64},{96,112},{112,96},{1... | collective-permute-start | bytes 9437192 | tf_op jit(solution)/shard_map/ppermute | solution.py:98
  85.9 5.1 %fusion.25 = f32[384,448]{0,1:T(8,128)} fusion(bf16[4096,448]{0,1:T(8,128)(2,1)} %param.13, bf16[384,4096]{0,1:T(8,128)(2,1)S(1)} %bitcast.84), kind=kOutput, calls=%fused_computation.80 | convolution fusion | flops 1409286144 | bytes 7503872 | tf_op jit(solution)/shard_map/dot_general | solution.py:101
  91.1 4.1 %fusion.26 = f32[384,448]{0,1:T(8,128)S(1)} fusion(bf16[4096,448]{0,1:T(8,128)(2,1)S(1)} %copy-done.5, bf16[384,4096]{0,1:T(8,128)(2,1)} %collective-permute-done.10), kind=kOutput, calls=%fused_computation.81 | convolution fusion | flops 1409286144 | bytes 7503872 | tf_op jit(solution)/shard_map/dot_general | solution.py:101
  95.2 4.7 %multiply_convert_fusion = bf16[384,448]{0,1:T(8,128)(2,1)} fusion(f32[384,448]{0,1:T(8,128)S(1)} %fusion.26, bf16[4096,448]{0,1:T(8,128)(2,1)S(1)} %copy-done.6, bf16[384,4096]{0,1:T(8,128)(2,1)} %collective-permute-done.10), kind=kOutput, calls=%fused_computation.12 | convolution fusion | flops 1410318336 | bytes 7847936 | tf_op jit(solution)/shard_map/dot_general | solution.py:102
  100.3 9.9 %fusion.1 = f32[384,4096]{1,0:T(8,128)} fusion(bf16[448,4096]{1,0:T(8,128)(2,1)} %param.15, bf16[4096,448]{0,1:T(8,128)(2,1)} %param.14, bf16[384,4096]{0,1:T(8,128)(2,1)S(1)} %bitcast.85, f32[384,448]{0,1:T(8,128)} %fusion.25), kind=kOutput, calls=%fused_computation.11 | convolution fusion | flops 2819604480 | bytes 17465344 | tf_op jit(solution)/shard_map/dot_general | solution.py:108
  110.2 5.7 %add_convert_fusion = bf16[384,4096]{1,0:T(8,128)(2,1)S(1)} fusion(f32[384,4096]{1,0:T(8,128)} %fusion.1, bf16[384,448]{0,1:T(8,128)(2,1)S(1)} %collective-permute-done.11, bf16[448,4096]{1,0:T(8,128)(2,1)} %collective-permute-done.12), kind=kOutput, calls=%fused_computation.6 | convolution fusion | flops 1412431872 | bytes 13451264 | tf_op jit(solution)/shard_map/dot_general | solution.py:108
  117.0 2.4 %copy.32 = bf16[384,2,8,256]{3,1,0,2:T(2,128)(2,1)S(1)} copy(bf16[384,2,8,256]{3,2,1,0:T(8,128)(2,1)S(1)} %bitcast.82) | data formatting | bytes 6291456 | tf_op jit(solution)/shard_map/reshape | solution.py:47
  119.4 2.2 %fusion.24 = (bf16[8,192,2,256]{3,2,1,0:T(2,128)(2,1)S(1)}, bf16[8,192,2,256]{3,2,1,0:T(2,128)(2,1)S(1)}) fusion(bf16[8,384,2,256]{3,2,1,0:T(2,128)(2,1)S(1)} %bitcast.81), kind=kLoop, calls=%fused_computation.79 | loop fusion | bytes 6291456 | tf_op jit(solution)/shard_map/slice | solution.py:48
  122.8 56.6 %while.18 = (s32[]{:T(128)}, f32[192,2,256]{2,1,0:T(2,128)S(1)}, f32[192,2,256]{2,1,0:T(2,128)S(1)}, s32[]{:T(128)}, bf16[8,192,2,256]{3,2,1,0:T(2,128)(2,1)}, /...) while((s32[]{:T(128)}, f32[192,2,256]{2,1,0:T(2,128)S(1)}, ...), condition=%wide.region_5.7_spmd, body=%wide.region_4.6_spmd.sunk | while | flops 786466 | bytes 4325915 | solution.py:59
  124.7 4.6 %collective-permute-done.1 = bf16[192,2,256]{2,1,0:T(2,128)(2,1)S(1)} collective-permute-done((bf16[192,2,256]{2,1,0:T(2,128)(2,1)S(1)}, bf16[192,2,256]{2,1,0:T(2,128)(2,1)S(1)}, u32[]{:S(2)}, u32[]{:S(2)}) %collective-permute-start.1) | collective-permute-done | bytes 196640 | tf_op jit(solution)/shard_map/while/body/eval_jaxpr/ppermute | solution.py:54
  133.8 3.8 %collective-permute-done.1 = bf16[192,2,256]{2,1,0:T(2,128)(2,1)S(1)} collective-permute-done((bf16[192,2,256]{2,1,0:T(2,128)(2,1)S(1)}, bf16[192,2,256]{2,1,0:T(2,128)(2,1)S(1)}, u32[]{:S(2)}, u32[]{:S(2)}) %collective-permute-start.1) | collective-permute-done | bytes 196640 | tf_op jit(solution)/shard_map/while/body/eval_jaxpr/ppermute | solution.py:54
  142.4 2.8 %collective-permute-done.1 = bf16[192,2,256]{2,1,0:T(2,128)(2,1)S(1)} collective-permute-done((bf16[192,2,256]{2,1,0:T(2,128)(2,1)S(1)}, bf16[192,2,256]{2,1,0:T(2,128)(2,1)S(1)}, u32[]{:S(2)}, u32[]{:S(2)}) %collective-permute-start.1) | collective-permute-done | bytes 196640 | tf_op jit(solution)/shard_map/while/body/eval_jaxpr/ppermute | solution.py:54
  150.0 2.8 %collective-permute-done.1 = bf16[192,2,256]{2,1,0:T(2,128)(2,1)S(1)} collective-permute-done((bf16[192,2,256]{2,1,0:T(2,128)(2,1)S(1)}, bf16[192,2,256]{2,1,0:T(2,128)(2,1)S(1)}, u32[]{:S(2)}, u32[]{:S(2)}) %collective-permute-start.1) | collective-permute-done | bytes 196640 | tf_op jit(solution)/shard_map/while/body/eval_jaxpr/ppermute | solution.py:54
  157.3 2.8 %collective-permute-done.1 = bf16[192,2,256]{2,1,0:T(2,128)(2,1)S(1)} collective-permute-done((bf16[192,2,256]{2,1,0:T(2,128)(2,1)S(1)}, bf16[192,2,256]{2,1,0:T(2,128)(2,1)S(1)}, u32[]{:S(2)}, u32[]{:S(2)}) %collective-permute-start.1) | collective-permute-done | bytes 196640 | tf_op jit(solution)/shard_map/while/body/eval_jaxpr/ppermute | solution.py:54
  165.0 2.8 %collective-permute-done.1 = bf16[192,2,256]{2,1,0:T(2,128)(2,1)S(1)} collective-permute-done((bf16[192,2,256]{2,1,0:T(2,128)(2,1)S(1)}, bf16[192,2,256]{2,1,0:T(2,128)(2,1)S(1)}, u32[]{:S(2)}, u32[]{:S(2)}) %collective-permute-start.1) | collective-permute-done | bytes 196640 | tf_op jit(solution)/shard_map/while/body/eval_jaxpr/ppermute | solution.py:54
  172.9 3.7 %collective-permute-done.1 = bf16[192,2,256]{2,1,0:T(2,128)(2,1)S(1)} collective-permute-done((bf16[192,2,256]{2,1,0:T(2,128)(2,1)S(1)}, bf16[192,2,256]{2,1,0:T(2,128)(2,1)S(1)}, u32[]{:S(2)}, u32[]{:S(2)}) %collective-permute-start.1) | collective-permute-done | bytes 196640 | tf_op jit(solution)/shard_map/while/body/eval_jaxpr/ppermute | solution.py:54
  179.9 4.5 %collective-permute-done.13 = bf16[384,256]{1,0:T(8,128)(2,1)S(1)} collective-permute-done((bf16[384,256]{1,0:T(8,128)(2,1)S(1)}, bf16[384,256]{1,0:T(8,128)(2,1)S(1)}, u32[]{:S(2)}, u32[]{:S(2)}) %collective-permute-start.13) | collective-permute-done | bytes 196640 | tf_op jit(solution)/shard_map/ppermute | solution.py:63
  185.1 14.7 %all-to-all-start.1 = ((bf16[16,24,256]{2,1,0:T(8,128)(2,1)}), bf16[16,24,256]{2,1,0:T(8,128)(2,1)S(1)}, u32[]{:S(2)}, u32[]{:S(2)}) async-start(bf16[16,24,256]{2,1,0:T(8,128)(2,1)} %bitcast.27), calls=%async_computation.1 | async-start | bytes 393216 | tf_op jit(solution)/shard_map/all_to_all | solution.py:112
  200.0 8.0 %all-to-all-done.1 = bf16[16,24,256]{2,1,0:T(8,128)(2,1)S(1)} async-done(((bf16[16,24,256]{2,1,0:T(8,128)(2,1)}), bf16[16,24,256]{2,1,0:T(8,128)(2,1)S(1)}, u32[]{:S(2)}, u32[]{:S(2)}) %all-to-all-start.1) | async-done | bytes 196640 | tf_op jit(solution)/shard_map/all_to_all | solution.py:112
  (123 shorter events, 52.9 us)
Async XLA Ops:
  0.0 5.1 %copy-start = (bf16[128,256]{1,0:T(8,128)(2,1)S(1)}, bf16[128,256]{1,0:T(8,128)(2,1)}, u32[]{:S(2)}) copy-start(bf16[128,256]{1,0:T(8,128)(2,1)} %param.10) | copy-start | bytes 196612
  23.7 5.7 %collective-permute-start.2 = (bf16[384,256]{1,0:T(8,128)(2,1)S(1)}, bf16[384,256]{1,0:T(8,128)(2,1)S(1)}, u32[]{:S(2)}, u32[]{:S(2)}) collective-permute-start(bf16[384,256]{1,0:T(8,128)(2,1)S(1)} %bitcast.86), channel_id=1, source_target_pairs={{0,8},{1,9},{2,10},{3,11},{4,12},{5,13},{6,14},{7,15},{8,0},{9,1},... | collective-permute-start | bytes 589832 | tf_op jit(solution)/shard_map/ppermute | solution.py:22
  29.4 13.5 %collective-permute-start.3 = (bf16[384,2,256]{2,0,1:T(8,128)(2,1)S(1)}, bf16[384,2,256]{2,0,1:T(8,128)(2,1)S(1)}, u32[]{:S(2)}, u32[]{:S(2)}) collective-permute-start(bf16[384,2,256]{2,0,1:T(8,128)(2,1)S(1)} %maximum_select_fusion.1), channel_id=1, source_target_pairs={{0,1},{1,2},{2,3},{3,4},{4,5},{5,6},{6,7},{7,0},{8,9},{9,10},{10,1... | collective-permute-start | bytes 1179656 | tf_op jit(solution)/shard_map/ppermute | solution.py:27
  31.1 11.8 %collective-permute-start.7 = (bf16[384,2,256]{2,0,1:T(8,128)(2,1)S(1)}, bf16[384,2,256]{2,0,1:T(8,128)(2,1)S(1)}, u32[]{:S(2)}, u32[]{:S(2)}) collective-permute-start(bf16[384,2,256]{2,0,1:T(8,128)(2,1)S(1)} %maximum_select_fusion.1), channel_id=1, source_target_pairs={{0,7},{1,0},{2,1},{3,2},{4,3},{5,4},{6,5},{7,6},{8,15},{9,8},{10,9... | collective-permute-start | bytes 1179656 | tf_op jit(solution)/shard_map/ppermute | solution.py:30
  42.9 9.7 %collective-permute-start.4 = (bf16[384,2,256]{2,0,1:T(8,128)(2,1)S(1)}, bf16[384,2,256]{2,0,1:T(8,128)(2,1)S(1)}, u32[]{:S(2)}, u32[]{:S(2)}) collective-permute-start(bf16[384,2,256]{2,0,1:T(8,128)(2,1)S(1)} %collective-permute-done.3), channel_id=1, source_target_pairs={{0,1},{1,2},{2,3},{3,4},{4,5},{5,6},{6,7},{7,0},{8,9},{9,10},{10,1... | collective-permute-start | bytes 1179656 | tf_op jit(solution)/shard_map/ppermute | solution.py:27
  42.9 11.2 %collective-permute-start.8 = (bf16[384,2,256]{2,0,1:T(8,128)(2,1)S(1)}, bf16[384,2,256]{2,0,1:T(8,128)(2,1)S(1)}, u32[]{:S(2)}, u32[]{:S(2)}) collective-permute-start(bf16[384,2,256]{2,0,1:T(8,128)(2,1)S(1)} %collective-permute-done.7), channel_id=1, source_target_pairs={{0,7},{1,0},{2,1},{3,2},{4,3},{5,4},{6,5},{7,6},{8,15},{9,8},{10,9... | collective-permute-start | bytes 1179656 | tf_op jit(solution)/shard_map/ppermute | solution.py:30
  52.6 8.8 %collective-permute-start.5 = (bf16[384,2,256]{2,0,1:T(8,128)(2,1)S(1)}, bf16[384,2,256]{2,0,1:T(8,128)(2,1)S(1)}, u32[]{:S(2)}, u32[]{:S(2)}) collective-permute-start(bf16[384,2,256]{2,0,1:T(8,128)(2,1)S(1)} %collective-permute-done.4), channel_id=1, source_target_pairs={{0,1},{1,2},{2,3},{3,4},{4,5},{5,6},{6,7},{7,0},{8,9},{9,10},{10,1... | collective-permute-start | bytes 1179656 | tf_op jit(solution)/shard_map/ppermute | solution.py:27
  54.2 15.8 %collective-permute-start.9 = (bf16[384,2,256]{2,0,1:T(8,128)(2,1)S(1)}, bf16[384,2,256]{2,0,1:T(8,128)(2,1)S(1)}, u32[]{:S(2)}, u32[]{:S(2)}) collective-permute-start(bf16[384,2,256]{2,0,1:T(8,128)(2,1)S(1)} %collective-permute-done.8), channel_id=1, source_target_pairs={{0,7},{1,0},{2,1},{3,2},{4,3},{5,4},{6,5},{7,6},{8,15},{9,8},{10,9... | collective-permute-start | bytes 1179656 | tf_op jit(solution)/shard_map/ppermute | solution.py:30
  61.4 7.8 %collective-permute-start.6 = (bf16[384,2,256]{2,0,1:T(8,128)(2,1)S(1)}, bf16[384,2,256]{2,0,1:T(8,128)(2,1)S(1)}, u32[]{:S(2)}, u32[]{:S(2)}) collective-permute-start(bf16[384,2,256]{2,0,1:T(8,128)(2,1)S(1)} %collective-permute-done.5), channel_id=1, source_target_pairs={{0,1},{1,2},{2,3},{3,4},{4,5},{5,6},{6,7},{7,0},{8,9},{9,10},{10,1... | collective-permute-start | bytes 1179656 | tf_op jit(solution)/shard_map/ppermute | solution.py:27
  80.5 10.6 %collective-permute-start.10 = (bf16[384,4096]{0,1:T(8,128)(2,1)S(1)}, bf16[384,4096]{0,1:T(8,128)(2,1)}, u32[]{:S(2)}, u32[]{:S(2)}) collective-permute-start(bf16[384,4096]{0,1:T(8,128)(2,1)S(1)} %bitcast.83), channel_id=1, source_target_pairs={{0,16},{16,0},{32,48},{48,32},{64,80},{80,64},{96,112},{112,96},{1... | collective-permute-start | bytes 9437192 | tf_op jit(solution)/shard_map/ppermute | solution.py:98
  85.6 24.5 %collective-permute-start.12 = (bf16[448,4096]{1,0:T(8,128)(2,1)}, bf16[448,4096]{1,0:T(8,128)(2,1)}, u32[]{:S(2)}, u32[]{:S(2)}) collective-permute-start(bf16[448,4096]{1,0:T(8,128)(2,1)} %param.15), channel_id=1, source_target_pairs={{0,16},{16,0},{32,48},{48,32},{64,80},{80,64},{96,112},{112,96},{1... | collective-permute-start | bytes 11010056 | tf_op jit(solution)/shard_map/ppermute | solution.py:97
  85.9 5.1 %copy-start.5 = (bf16[4096,448]{0,1:T(8,128)(2,1)S(1)}, bf16[4096,448]{0,1:T(8,128)(2,1)}, u32[]{:S(2)}) copy-start(bf16[4096,448]{0,1:T(8,128)(2,1)} %param.13) | copy-start | bytes 11010052
  91.0 4.1 %copy-start.6 = (bf16[4096,448]{0,1:T(8,128)(2,1)S(1)}, bf16[4096,448]{0,1:T(8,128)(2,1)}, u32[]{:S(2)}) copy-start(bf16[4096,448]{0,1:T(8,128)(2,1)} %param.14) | copy-start | bytes 11010052
  99.9 10.2 %collective-permute-start.11 = (bf16[384,448]{0,1:T(8,128)(2,1)}, bf16[384,448]{0,1:T(8,128)(2,1)S(1)}, u32[]{:S(2)}, u32[]{:S(2)}) collective-permute-start(bf16[384,448]{0,1:T(8,128)(2,1)} %multiply_convert_fusion), channel_id=1, source_target_pairs={{0,16},{16,0},{32,48},{48,32},{64,80},{80,64},{96,112},{112,96},{1... | collective-permute-start | bytes 1032200 | tf_op jit(solution)/shard_map/ppermute | solution.py:107
  122.8 57.1 %copy-start.4 = (s32[128,2]{0,1:T(2,128)S(1)}, s32[128,2]{0,1:T(2,128)}, u32[]{:S(2)}) copy-start(s32[128,2]{0,1:T(2,128)} %param.12) | copy-start | bytes 3076
  122.9 6.4 %collective-permute-start.1 = (bf16[192,2,256]{2,1,0:T(2,128)(2,1)S(1)}, bf16[192,2,256]{2,1,0:T(2,128)(2,1)S(1)}, u32[]{:S(2)}, u32[]{:S(2)}) collective-permute-start(bf16[192,2,256]{2,1,0:T(2,128)(2,1)S(1)} %convert_element_type.155), channel_id=1, source_target_pairs={{0,7},{1,0},{2,1},{3,2},{4,3},{5,4},{6,5},{7,6},{8,15},{9,8},{10,9... | collective-permute-start | bytes 589832 | tf_op jit(solution)/shard_map/while/body/eval_jaxpr/ppermute | solution.py:54
  123.2 7.6 %collective-permute-start = (bf16[192,2,256]{2,1,0:T(2,128)(2,1)S(1)}, bf16[192,2,256]{2,1,0:T(2,128)(2,1)S(1)}, u32[]{:S(2)}, u32[]{:S(2)}) collective-permute-start(bf16[192,2,256]{2,1,0:T(2,128)(2,1)S(1)} %convert_element_type.154), channel_id=1, source_target_pairs={{0,1},{1,2},{2,3},{3,4},{4,5},{5,6},{6,7},{7,0},{8,9},{9,10},{10,1... | collective-permute-start | bytes 589832 | tf_op jit(solution)/shard_map/while/body/eval_jaxpr/ppermute | solution.py:53
  132.1 5.5 %collective-permute-start.1 = (bf16[192,2,256]{2,1,0:T(2,128)(2,1)S(1)}, bf16[192,2,256]{2,1,0:T(2,128)(2,1)S(1)}, u32[]{:S(2)}, u32[]{:S(2)}) collective-permute-start(bf16[192,2,256]{2,1,0:T(2,128)(2,1)S(1)} %convert_element_type.155), channel_id=1, source_target_pairs={{0,7},{1,0},{2,1},{3,2},{4,3},{5,4},{6,5},{7,6},{8,15},{9,8},{10,9... | collective-permute-start | bytes 589832 | tf_op jit(solution)/shard_map/while/body/eval_jaxpr/ppermute | solution.py:54
  132.6 6.8 %collective-permute-start = (bf16[192,2,256]{2,1,0:T(2,128)(2,1)S(1)}, bf16[192,2,256]{2,1,0:T(2,128)(2,1)S(1)}, u32[]{:S(2)}, u32[]{:S(2)}) collective-permute-start(bf16[192,2,256]{2,1,0:T(2,128)(2,1)S(1)} %convert_element_type.154), channel_id=1, source_target_pairs={{0,1},{1,2},{2,3},{3,4},{4,5},{5,6},{6,7},{7,0},{8,9},{9,10},{10,1... | collective-permute-start | bytes 589832 | tf_op jit(solution)/shard_map/while/body/eval_jaxpr/ppermute | solution.py:53
  140.6 4.6 %collective-permute-start.1 = (bf16[192,2,256]{2,1,0:T(2,128)(2,1)S(1)}, bf16[192,2,256]{2,1,0:T(2,128)(2,1)S(1)}, u32[]{:S(2)}, u32[]{:S(2)}) collective-permute-start(bf16[192,2,256]{2,1,0:T(2,128)(2,1)S(1)} %convert_element_type.155), channel_id=1, source_target_pairs={{0,7},{1,0},{2,1},{3,2},{4,3},{5,4},{6,5},{7,6},{8,15},{9,8},{10,9... | collective-permute-start | bytes 589832 | tf_op jit(solution)/shard_map/while/body/eval_jaxpr/ppermute | solution.py:54
  141.1 5.8 %collective-permute-start = (bf16[192,2,256]{2,1,0:T(2,128)(2,1)S(1)}, bf16[192,2,256]{2,1,0:T(2,128)(2,1)S(1)}, u32[]{:S(2)}, u32[]{:S(2)}) collective-permute-start(bf16[192,2,256]{2,1,0:T(2,128)(2,1)S(1)} %convert_element_type.154), channel_id=1, source_target_pairs={{0,1},{1,2},{2,3},{3,4},{4,5},{5,6},{6,7},{7,0},{8,9},{9,10},{10,1... | collective-permute-start | bytes 589832 | tf_op jit(solution)/shard_map/while/body/eval_jaxpr/ppermute | solution.py:53
  148.2 4.6 %collective-permute-start.1 = (bf16[192,2,256]{2,1,0:T(2,128)(2,1)S(1)}, bf16[192,2,256]{2,1,0:T(2,128)(2,1)S(1)}, u32[]{:S(2)}, u32[]{:S(2)}) collective-permute-start(bf16[192,2,256]{2,1,0:T(2,128)(2,1)S(1)} %convert_element_type.155), channel_id=1, source_target_pairs={{0,7},{1,0},{2,1},{3,2},{4,3},{5,4},{6,5},{7,6},{8,15},{9,8},{10,9... | collective-permute-start | bytes 589832 | tf_op jit(solution)/shard_map/while/body/eval_jaxpr/ppermute | solution.py:54
  148.5 5.8 %collective-permute-start = (bf16[192,2,256]{2,1,0:T(2,128)(2,1)S(1)}, bf16[192,2,256]{2,1,0:T(2,128)(2,1)S(1)}, u32[]{:S(2)}, u32[]{:S(2)}) collective-permute-start(bf16[192,2,256]{2,1,0:T(2,128)(2,1)S(1)} %convert_element_type.154), channel_id=1, source_target_pairs={{0,1},{1,2},{2,3},{3,4},{4,5},{5,6},{6,7},{7,0},{8,9},{9,10},{10,1... | collective-permute-start | bytes 589832 | tf_op jit(solution)/shard_map/while/body/eval_jaxpr/ppermute | solution.py:53
  155.6 4.6 %collective-permute-start.1 = (bf16[192,2,256]{2,1,0:T(2,128)(2,1)S(1)}, bf16[192,2,256]{2,1,0:T(2,128)(2,1)S(1)}, u32[]{:S(2)}, u32[]{:S(2)}) collective-permute-start(bf16[192,2,256]{2,1,0:T(2,128)(2,1)S(1)} %convert_element_type.155), channel_id=1, source_target_pairs={{0,7},{1,0},{2,1},{3,2},{4,3},{5,4},{6,5},{7,6},{8,15},{9,8},{10,9... | collective-permute-start | bytes 589832 | tf_op jit(solution)/shard_map/while/body/eval_jaxpr/ppermute | solution.py:54
  156.2 5.8 %collective-permute-start = (bf16[192,2,256]{2,1,0:T(2,128)(2,1)S(1)}, bf16[192,2,256]{2,1,0:T(2,128)(2,1)S(1)}, u32[]{:S(2)}, u32[]{:S(2)}) collective-permute-start(bf16[192,2,256]{2,1,0:T(2,128)(2,1)S(1)} %convert_element_type.154), channel_id=1, source_target_pairs={{0,1},{1,2},{2,3},{3,4},{4,5},{5,6},{6,7},{7,0},{8,9},{9,10},{10,1... | collective-permute-start | bytes 589832 | tf_op jit(solution)/shard_map/while/body/eval_jaxpr/ppermute | solution.py:53
  163.3 4.6 %collective-permute-start.1 = (bf16[192,2,256]{2,1,0:T(2,128)(2,1)S(1)}, bf16[192,2,256]{2,1,0:T(2,128)(2,1)S(1)}, u32[]{:S(2)}, u32[]{:S(2)}) collective-permute-start(bf16[192,2,256]{2,1,0:T(2,128)(2,1)S(1)} %convert_element_type.155), channel_id=1, source_target_pairs={{0,7},{1,0},{2,1},{3,2},{4,3},{5,4},{6,5},{7,6},{8,15},{9,8},{10,9... | collective-permute-start | bytes 589832 | tf_op jit(solution)/shard_map/while/body/eval_jaxpr/ppermute | solution.py:54
  164.0 5.8 %collective-permute-start = (bf16[192,2,256]{2,1,0:T(2,128)(2,1)S(1)}, bf16[192,2,256]{2,1,0:T(2,128)(2,1)S(1)}, u32[]{:S(2)}, u32[]{:S(2)}) collective-permute-start(bf16[192,2,256]{2,1,0:T(2,128)(2,1)S(1)} %convert_element_type.154), channel_id=1, source_target_pairs={{0,1},{1,2},{2,3},{3,4},{4,5},{5,6},{6,7},{7,0},{8,9},{9,10},{10,1... | collective-permute-start | bytes 589832 | tf_op jit(solution)/shard_map/while/body/eval_jaxpr/ppermute | solution.py:53
  171.1 5.4 %collective-permute-start.1 = (bf16[192,2,256]{2,1,0:T(2,128)(2,1)S(1)}, bf16[192,2,256]{2,1,0:T(2,128)(2,1)S(1)}, u32[]{:S(2)}, u32[]{:S(2)}) collective-permute-start(bf16[192,2,256]{2,1,0:T(2,128)(2,1)S(1)} %convert_element_type.155), channel_id=1, source_target_pairs={{0,7},{1,0},{2,1},{3,2},{4,3},{5,4},{6,5},{7,6},{8,15},{9,8},{10,9... | collective-permute-start | bytes 589832 | tf_op jit(solution)/shard_map/while/body/eval_jaxpr/ppermute | solution.py:54
  171.4 6.9 %collective-permute-start = (bf16[192,2,256]{2,1,0:T(2,128)(2,1)S(1)}, bf16[192,2,256]{2,1,0:T(2,128)(2,1)S(1)}, u32[]{:S(2)}, u32[]{:S(2)}) collective-permute-start(bf16[192,2,256]{2,1,0:T(2,128)(2,1)S(1)} %convert_element_type.154), channel_id=1, source_target_pairs={{0,1},{1,2},{2,3},{3,4},{4,5},{5,6},{6,7},{7,0},{8,9},{9,10},{10,1... | collective-permute-start | bytes 589832 | tf_op jit(solution)/shard_map/while/body/eval_jaxpr/ppermute | solution.py:53
  179.4 20.6 %copy-start.3 = (s32[256,1]{0,1:T(1,128)S(1)}, s32[256,1]{0,1:T(1,128)}, u32[]{:S(2)}) copy-start(s32[256,1]{0,1:T(1,128)} %copy-done.2) | copy-start | bytes 3076
  179.5 4.9 %collective-permute-start.13 = (bf16[384,256]{1,0:T(8,128)(2,1)S(1)}, bf16[384,256]{1,0:T(8,128)(2,1)S(1)}, u32[]{:S(2)}, u32[]{:S(2)}) collective-permute-start(bf16[384,256]{1,0:T(8,128)(2,1)S(1)} %fusion.14), channel_id=1, source_target_pairs={{0,8},{1,9},{2,10},{3,11},{4,12},{5,13},{6,14},{7,15},{8,0},{9,1},... | collective-permute-start | bytes 589832 | tf_op jit(solution)/shard_map/ppermute | solution.py:63
  185.1 22.9 %all-to-all-start.1 = ((bf16[16,24,256]{2,1,0:T(8,128)(2,1)}), bf16[16,24,256]{2,1,0:T(8,128)(2,1)S(1)}, u32[]{:S(2)}, u32[]{:S(2)}) async-start(bf16[16,24,256]{2,1,0:T(8,128)(2,1)} %bitcast.27), calls=%async_computation.1 | async-start | bytes 393216 | tf_op jit(solution)/shard_map/all_to_all | solution.py:112
  (2 other events, 1.7 us)

commit v2 on v0

--- a/solution.py
+++ b/solution.py
@@ -101,9 +101,8 @@
     h_mine = hidden_of(x_mine)
     h_other = hidden_of(x_other)
     h_back = lax.ppermute(h_other, "dp", pairs)
-    both = jnp.dot(h_mine, w_down, preferred_element_type=jnp.float32) + jnp.dot(
-        h_back, w_down_partner, preferred_element_type=jnp.float32
-    )
+    p_own = lax.optimization_barrier(jnp.dot(h_mine, w_down, preferred_element_type=jnp.float32).astype(jnp.bfloat16))
+    both = p_own.astype(jnp.float32) + jnp.dot(h_back, w_down_partner, preferred_element_type=jnp.float32)
     summed = scatter_hid(both.astype(jnp.bfloat16))
     returned = lax.all_to_all(
         summed.reshape(devices_dp, part_cap, chunk), "dp", split_axis=0, concat_axis=0, tiled=True

time: 197 us -> 195 us (0.990)
  no operation moved by 1% of the time
where the time goes in v2:
time: 195 us
  waiting for transfers between devices  69.2 us (35%)
  starting transfers between devices  51.6 us (26%)
  matrix products  27.6 us (14%)
  local copies, waits for them, and re-layouts  20.9 us (11%)
  blocking collectives  16.4 us (8%)
  other arithmetic  8.26 us (4%)
    ppermute x7, waiting for transfers between devices, scatter_hid(): ra = lax.ppermute(a.astype(jnp.bfloat16), 'hid', cw)  25.9 us
    ppermute x4, waiting for transfers between devices, gather_hid(): a = lax.ppermute(a, 'hid', cw)  25.4 us
    ppermute x7, starting transfers between devices, scatter_hid(): rb = lax.ppermute(b.astype(jnp.bfloat16), 'hid', ccw)  19 us
    all_to_all x1, blocking collectives, local(): lax.all_to_all(picked, 'dp', split_axis=0, concat_axis=0, tiled=True)  16.4 us
    all_to_all x1, starting transfers between devices, local(): lax.all_to_all(summed.reshape(devices_dp, part_cap, chunk), 'dp', split_a...  14.1 us
    ppermute x3, starting transfers between devices, gather_hid(): b = lax.ppermute(b, 'hid', ccw)  9.45 us
    dot_general x2, matrix products, hidden_of(): gate = jnp.dot(x, w_gate, preferred_element_type=jnp.float32)  9.2 us
    dot_general x1, matrix products, local(): jnp.dot(h_mine, w_down, preferred_element_type=jnp.float32)  8.88 us
  transfers between devices with their start and end apart: 27, of which 14 were waited for; matrix products, arithmetic and copies ran while one was open for 15% of the time, Pallas kernels for 0%

profile of v2, /device:TPU:1, one launch (start us, length us, event | category | flops | bytes accessed | tf_op | source)
XLA Modules:
  0.0 194.8 jit_solution(7211673446290645922)
XLA Ops:
  7.3 16.4 %all_to_all.10 = bf16[16,24,256]{2,1,0:T(8,128)(2,1)S(1)} all-to-all(bf16[16,24,256]{2,1,0:T(8,128)(2,1)S(1)} %broadcast_select_fusion), channel_id=1, replica_groups=mesh['dp'=16,'hid'=16] {'dp'}, dimensions={0} | all-to-all | bytes 393216 | tf_op jit(solution)/shard_map/all_to_all | solution.py:88
  24.0 5.4 %collective-permute-done = bf16[384,256]{1,0:T(8,128)(2,1)S(1)} collective-permute-done((bf16[384,256]{1,0:T(8,128)(2,1)S(1)}, bf16[384,256]{1,0:T(8,128)(2,1)S(1)}, u32[]{:S(2)}, u32[]{:S(2)}) %collective-permute-start) | collective-permute-done | bytes 196640 | tf_op jit(solution)/shard_map/ppermute | solution.py:22
  31.1 4.0 %collective-permute-start.5 = (bf16[384,2,256]{2,0,1:T(8,128)(2,1)S(1)}, bf16[384,2,256]{2,0,1:T(8,128)(2,1)S(1)}, u32[]{:S(2)}, u32[]{:S(2)}) collective-permute-start(bf16[384,2,256]{2,0,1:T(8,128)(2,1)S(1)} %maximum_select_fusion.1), channel_id=1, source_target_pairs={{0,7},{1,0},{2,1},{3,2},{4,3},{5,4},{6,5},{7,6},{8,15},{9,8},{10,9... | collective-permute-start | bytes 1179656 | tf_op jit(solution)/shard_map/ppermute | solution.py:30
  35.1 7.8 %collective-permute-done.1 = bf16[384,2,256]{2,0,1:T(8,128)(2,1)S(1)} collective-permute-done((bf16[384,2,256]{2,0,1:T(8,128)(2,1)S(1)}, bf16[384,2,256]{2,0,1:T(8,128)(2,1)S(1)}, u32[]{:S(2)}, u32[]{:S(2)}) %collective-permute-start.1) | collective-permute-done | bytes 393248 | tf_op jit(solution)/shard_map/ppermute | solution.py:27
  42.9 2.7 %collective-permute-start.6 = (bf16[384,2,256]{2,0,1:T(8,128)(2,1)S(1)}, bf16[384,2,256]{2,0,1:T(8,128)(2,1)S(1)}, u32[]{:S(2)}, u32[]{:S(2)}) collective-permute-start(bf16[384,2,256]{2,0,1:T(8,128)(2,1)S(1)} %collective-permute-done.5), channel_id=1, source_target_pairs={{0,7},{1,0},{2,1},{3,2},{4,3},{5,4},{6,5},{7,6},{8,15},{9,8},{10,9... | collective-permute-start | bytes 1179656 | tf_op jit(solution)/shard_map/ppermute | solution.py:30
  45.7 6.9 %collective-permute-done.2 = bf16[384,2,256]{2,0,1:T(8,128)(2,1)S(1)} collective-permute-done((bf16[384,2,256]{2,0,1:T(8,128)(2,1)S(1)}, bf16[384,2,256]{2,0,1:T(8,128)(2,1)S(1)}, u32[]{:S(2)}, u32[]{:S(2)}) %collective-permute-start.2) | collective-permute-done | bytes 393248 | tf_op jit(solution)/shard_map/ppermute | solution.py:27
  54.2 2.7 %collective-permute-start.7 = (bf16[384,2,256]{2,0,1:T(8,128)(2,1)S(1)}, bf16[384,2,256]{2,0,1:T(8,128)(2,1)S(1)}, u32[]{:S(2)}, u32[]{:S(2)}) collective-permute-start(bf16[384,2,256]{2,0,1:T(8,128)(2,1)S(1)} %collective-permute-done.6), channel_id=1, source_target_pairs={{0,7},{1,0},{2,1},{3,2},{4,3},{5,4},{6,5},{7,6},{8,15},{9,8},{10,9... | collective-permute-start | bytes 1179656 | tf_op jit(solution)/shard_map/ppermute | solution.py:30
  56.8 4.5 %collective-permute-done.3 = bf16[384,2,256]{2,0,1:T(8,128)(2,1)S(1)} collective-permute-done((bf16[384,2,256]{2,0,1:T(8,128)(2,1)S(1)}, bf16[384,2,256]{2,0,1:T(8,128)(2,1)S(1)}, u32[]{:S(2)}, u32[]{:S(2)}) %collective-permute-start.3) | collective-permute-done | bytes 393248 | tf_op jit(solution)/shard_map/ppermute | solution.py:27
  62.9 6.3 %collective-permute-done.4 = bf16[384,2,256]{2,0,1:T(8,128)(2,1)S(1)} collective-permute-done((bf16[384,2,256]{2,0,1:T(8,128)(2,1)S(1)}, bf16[384,2,256]{2,0,1:T(8,128)(2,1)S(1)}, u32[]{:S(2)}, u32[]{:S(2)}) %collective-permute-start.4) | collective-permute-done | bytes 393248 | tf_op jit(solution)/shard_map/ppermute | solution.py:27
  77.0 3.4 %copy.28 = bf16[384,2,8,256]{0,3,2,1:T(8,128)(2,1)S(1)} copy(bf16[384,2,8,256]{3,0,1,2:T(8,128)(2,1)} %select_bitcast_fusion) | data formatting | bytes 6291456 | tf_op jit(solution)/shard_map/jit(_take)/select_n | solution.py:34
  80.4 5.2 %collective-permute-start.8 = (bf16[384,4096]{0,1:T(8,128)(2,1)S(1)}, bf16[384,4096]{0,1:T(8,128)(2,1)}, u32[]{:S(2)}, u32[]{:S(2)}) collective-permute-start(bf16[384,4096]{0,1:T(8,128)(2,1)S(1)} %bitcast.97), channel_id=1, source_target_pairs={{0,16},{16,0},{32,48},{48,32},{64,80},{80,64},{96,112},{112,96},{1... | collective-permute-start | bytes 9437192 | tf_op jit(solution)/shard_map/ppermute | solution.py:94
  85.9 5.1 %fusion.16 = f32[384,448]{0,1:T(8,128)} fusion(bf16[4096,448]{0,1:T(8,128)(2,1)} %param.11, bf16[384,4096]{0,1:T(8,128)(2,1)S(1)} %bitcast.98), kind=kOutput, calls=%fused_computation.85 | convolution fusion | flops 1409286144 | bytes 7503872 | tf_op jit(solution)/shard_map/dot_general | solution.py:97
  91.0 4.1 %fusion.17 = f32[384,448]{0,1:T(8,128)S(1)} fusion(bf16[4096,448]{0,1:T(8,128)(2,1)S(1)} %copy-done.4, bf16[384,4096]{0,1:T(8,128)(2,1)} %collective-permute-done.8), kind=kOutput, calls=%fused_computation.86 | convolution fusion | flops 1409286144 | bytes 7503872 | tf_op jit(solution)/shard_map/dot_general | solution.py:97
  95.1 4.7 %multiply_convert_fusion = bf16[384,448]{0,1:T(8,128)(2,1)} fusion(f32[384,448]{0,1:T(8,128)S(1)} %fusion.17, bf16[4096,448]{0,1:T(8,128)(2,1)S(1)} %copy-done.5, bf16[384,4096]{0,1:T(8,128)(2,1)} %collective-permute-done.8), kind=kOutput, calls=%fused_computation.12 | convolution fusion | flops 1410318336 | bytes 7847936 | tf_op jit(solution)/shard_map/dot_general | solution.py:98
  100.2 8.9 %convolution_convert_fusion = bf16[384,4096]{1,0:T(8,128)(2,1)} fusion(bf16[448,4096]{1,0:T(8,128)(2,1)} %param.13, bf16[4096,448]{0,1:T(8,128)(2,1)} %param.12, bf16[384,4096]{0,1:T(8,128)(2,1)S(1)} %bitcast.99, f32[384,448]{0,1:T(8,128)} %fusion.16), kind=kOutput, calls=%fused_computation.5 | convolution fusion | flops 2821177344 | bytes 14319616 | tf_op jit(solution)/shard_map/dot_general | solution.py:104
  109.1 4.8 %add_convert_fusion = bf16[384,4096]{1,0:T(8,128)(2,1)S(1)} fusion(bf16[384,4096]{1,0:T(8,128)(2,1)} %convolution_convert_fusion, bf16[384,448]{0,1:T(8,128)(2,1)S(1)} %collective-permute-done.9, bf16[448,4096]{1,0:T(8,128)(2,1)} %collective-permute-done.10), kind=kOutput, calls=%fused_computation.4 | convolution fusion | flops 1414004736 | bytes 10305536 | tf_op jit(solution)/shard_map/dot_general | solution.py:105
  119.5 4.9 %collective-permute-done.11 = bf16[192,2,256]{2,0,1:T(8,128)(2,1)} collective-permute-done((bf16[192,2,256]{2,0,1:T(8,128)(2,1)S(1)}, bf16[192,2,256]{2,0,1:T(8,128)(2,1)}, u32[]{:S(2)}, u32[]{:S(2)}) %collective-permute-start.11) | collective-permute-done | bytes 196640 | tf_op jit(solution)/shard_map/ppermute | solution.py:52
  125.6 2.7 %collective-permute-start.19 = (bf16[192,2,256]{2,0,1:T(8,128)(2,1)S(1)}, bf16[192,2,256]{2,0,1:T(8,128)(2,1)S(1)}, u32[]{:S(2)}, u32[]{:S(2)}) collective-permute-start(bf16[192,2,256]{2,0,1:T(8,128)(2,1)S(1)} %add_convert_fusion.6), channel_id=1, source_target_pairs={{0,7},{1,0},{2,1},{3,2},{4,3},{5,4},{6,5},{7,6},{8,15},{9,8},{10,9... | collective-permute-start | bytes 589832 | tf_op jit(solution)/shard_map/ppermute | solution.py:53
  128.3 3.9 %collective-permute-done.12 = bf16[192,2,256]{2,0,1:T(8,128)(2,1)S(1)} collective-permute-done((bf16[192,2,256]{2,0,1:T(8,128)(2,1)S(1)}, bf16[192,2,256]{2,0,1:T(8,128)(2,1)S(1)}, u32[]{:S(2)}, u32[]{:S(2)}) %collective-permute-start.12) | collective-permute-done | bytes 196640 | tf_op jit(solution)/shard_map/ppermute | solution.py:52
  132.4 2.7 %collective-permute-start.20 = (bf16[192,2,256]{2,0,1:T(8,128)(2,1)S(1)}, bf16[192,2,256]{2,0,1:T(8,128)(2,1)S(1)}, u32[]{:S(2)}, u32[]{:S(2)}) collective-permute-start(bf16[192,2,256]{2,0,1:T(8,128)(2,1)S(1)} %add_convert_fusion.5), channel_id=1, source_target_pairs={{0,7},{1,0},{2,1},{3,2},{4,3},{5,4},{6,5},{7,6},{8,15},{9,8},{10,9... | collective-permute-start | bytes 589832 | tf_op jit(solution)/shard_map/ppermute | solution.py:53
  135.1 2.9 %collective-permute-done.13 = bf16[192,2,256]{2,0,1:T(8,128)(2,1)S(1)} collective-permute-done((bf16[192,2,256]{2,0,1:T(8,128)(2,1)S(1)}, bf16[192,2,256]{2,0,1:T(8,128)(2,1)S(1)}, u32[]{:S(2)}, u32[]{:S(2)}) %collective-permute-start.13) | collective-permute-done | bytes 196640 | tf_op jit(solution)/shard_map/ppermute | solution.py:52
  138.3 2.7 %collective-permute-start.21 = (bf16[192,2,256]{2,0,1:T(8,128)(2,1)S(1)}, bf16[192,2,256]{2,0,1:T(8,128)(2,1)S(1)}, u32[]{:S(2)}, u32[]{:S(2)}) collective-permute-start(bf16[192,2,256]{2,0,1:T(8,128)(2,1)S(1)} %add_convert_fusion.4), channel_id=1, source_target_pairs={{0,7},{1,0},{2,1},{3,2},{4,3},{5,4},{6,5},{7,6},{8,15},{9,8},{10,9... | collective-permute-start | bytes 589832 | tf_op jit(solution)/shard_map/ppermute | solution.py:53
  141.0 2.9 %collective-permute-done.14 = bf16[192,2,256]{2,0,1:T(8,128)(2,1)S(1)} collective-permute-done((bf16[192,2,256]{2,0,1:T(8,128)(2,1)S(1)}, bf16[192,2,256]{2,0,1:T(8,128)(2,1)S(1)}, u32[]{:S(2)}, u32[]{:S(2)}) %collective-permute-start.14) | collective-permute-done | bytes 196640 | tf_op jit(solution)/shard_map/ppermute | solution.py:52
  144.2 2.7 %collective-permute-start.22 = (bf16[192,2,256]{2,0,1:T(8,128)(2,1)S(1)}, bf16[192,2,256]{2,0,1:T(8,128)(2,1)S(1)}, u32[]{:S(2)}, u32[]{:S(2)}) collective-permute-start(bf16[192,2,256]{2,0,1:T(8,128)(2,1)S(1)} %add_convert_fusion.3), channel_id=1, source_target_pairs={{0,7},{1,0},{2,1},{3,2},{4,3},{5,4},{6,5},{7,6},{8,15},{9,8},{10,9... | collective-permute-start | bytes 589832 | tf_op jit(solution)/shard_map/ppermute | solution.py:53
  146.9 2.9 %collective-permute-done.15 = bf16[192,2,256]{2,0,1:T(8,128)(2,1)S(1)} collective-permute-done((bf16[192,2,256]{2,0,1:T(8,128)(2,1)S(1)}, bf16[192,2,256]{2,0,1:T(8,128)(2,1)S(1)}, u32[]{:S(2)}, u32[]{:S(2)}) %collective-permute-start.15) | collective-permute-done | bytes 196640 | tf_op jit(solution)/shard_map/ppermute | solution.py:52
  150.0 2.7 %collective-permute-start.23 = (bf16[192,2,256]{2,0,1:T(8,128)(2,1)S(1)}, bf16[192,2,256]{2,0,1:T(8,128)(2,1)S(1)}, u32[]{:S(2)}, u32[]{:S(2)}) collective-permute-start(bf16[192,2,256]{2,0,1:T(8,128)(2,1)S(1)} %add_convert_fusion.2), channel_id=1, source_target_pairs={{0,7},{1,0},{2,1},{3,2},{4,3},{5,4},{6,5},{7,6},{8,15},{9,8},{10,9... | collective-permute-start | bytes 589832 | tf_op jit(solution)/shard_map/ppermute | solution.py:53
  152.8 3.7 %collective-permute-done.16 = bf16[192,2,256]{2,0,1:T(8,128)(2,1)S(1)} collective-permute-done((bf16[192,2,256]{2,0,1:T(8,128)(2,1)S(1)}, bf16[192,2,256]{2,0,1:T(8,128)(2,1)S(1)}, u32[]{:S(2)}, u32[]{:S(2)}) %collective-permute-start.16) | collective-permute-done | bytes 196640 | tf_op jit(solution)/shard_map/ppermute | solution.py:52
  156.7 3.0 %collective-permute-start.24 = (bf16[192,2,256]{2,0,1:T(8,128)(2,1)S(1)}, bf16[192,2,256]{2,0,1:T(8,128)(2,1)S(1)}, u32[]{:S(2)}, u32[]{:S(2)}) collective-permute-start(bf16[192,2,256]{2,0,1:T(8,128)(2,1)S(1)} %add_convert_fusion.1), channel_id=1, source_target_pairs={{0,7},{1,0},{2,1},{3,2},{4,3},{5,4},{6,5},{7,6},{8,15},{9,8},{10,9... | collective-permute-start | bytes 589832 | tf_op jit(solution)/shard_map/ppermute | solution.py:53
  159.8 4.7 %collective-permute-done.17 = bf16[192,2,256]{2,0,1:T(8,128)(2,1)S(1)} collective-permute-done((bf16[192,2,256]{2,0,1:T(8,128)(2,1)S(1)}, bf16[192,2,256]{2,0,1:T(8,128)(2,1)S(1)}, u32[]{:S(2)}, u32[]{:S(2)}) %collective-permute-start.17) | collective-permute-done | bytes 196640 | tf_op jit(solution)/shard_map/ppermute | solution.py:52
  165.1 4.5 %collective-permute-done.25 = bf16[384,256]{1,0:T(8,128)(2,1)S(1)} collective-permute-done((bf16[384,256]{1,0:T(8,128)(2,1)S(1)}, bf16[384,256]{1,0:T(8,128)(2,1)S(1)}, u32[]{:S(2)}, u32[]{:S(2)}) %collective-permute-start.25) | collective-permute-done | bytes 196640 | tf_op jit(solution)/shard_map/ppermute | solution.py:59
  170.4 14.1 %all-to-all-start.1 = ((bf16[16,24,256]{2,1,0:T(8,128)(2,1)}), bf16[16,24,256]{2,1,0:T(8,128)(2,1)S(1)}, u32[]{:S(2)}, u32[]{:S(2)}) async-start(bf16[16,24,256]{2,1,0:T(8,128)(2,1)} %bitcast.39), calls=%async_computation.1 | async-start | bytes 393216 | tf_op jit(solution)/shard_map/all_to_all | solution.py:107
  184.6 8.0 %all-to-all-done.1 = bf16[16,24,256]{2,1,0:T(8,128)(2,1)S(1)} async-done(((bf16[16,24,256]{2,1,0:T(8,128)(2,1)}), bf16[16,24,256]{2,1,0:T(8,128)(2,1)S(1)}, u32[]{:S(2)}, u32[]{:S(2)}) %all-to-all-start.1) | async-done | bytes 196640 | tf_op jit(solution)/shard_map/all_to_all | solution.py:107
  (105 shorter events, 32.0 us)
Async XLA Ops:
  0.0 5.1 %copy-start = (bf16[128,256]{1,0:T(8,128)(2,1)S(1)}, bf16[128,256]{1,0:T(8,128)(2,1)}, u32[]{:S(2)}) copy-start(bf16[128,256]{1,0:T(8,128)(2,1)} %param.8) | copy-start | bytes 196612
  23.7 5.7 %collective-permute-start = (bf16[384,256]{1,0:T(8,128)(2,1)S(1)}, bf16[384,256]{1,0:T(8,128)(2,1)S(1)}, u32[]{:S(2)}, u32[]{:S(2)}) collective-permute-start(bf16[384,256]{1,0:T(8,128)(2,1)S(1)} %bitcast.100), channel_id=1, source_target_pairs={{0,8},{1,9},{2,10},{3,11},{4,12},{5,13},{6,14},{7,15},{8,0},{9,1},... | collective-permute-start | bytes 589832 | tf_op jit(solution)/shard_map/ppermute | solution.py:22
  29.4 13.5 %collective-permute-start.1 = (bf16[384,2,256]{2,0,1:T(8,128)(2,1)S(1)}, bf16[384,2,256]{2,0,1:T(8,128)(2,1)S(1)}, u32[]{:S(2)}, u32[]{:S(2)}) collective-permute-start(bf16[384,2,256]{2,0,1:T(8,128)(2,1)S(1)} %maximum_select_fusion.1), channel_id=1, source_target_pairs={{0,1},{1,2},{2,3},{3,4},{4,5},{5,6},{6,7},{7,0},{8,9},{9,10},{10,1... | collective-permute-start | bytes 1179656 | tf_op jit(solution)/shard_map/ppermute | solution.py:27
  31.1 11.8 %collective-permute-start.5 = (bf16[384,2,256]{2,0,1:T(8,128)(2,1)S(1)}, bf16[384,2,256]{2,0,1:T(8,128)(2,1)S(1)}, u32[]{:S(2)}, u32[]{:S(2)}) collective-permute-start(bf16[384,2,256]{2,0,1:T(8,128)(2,1)S(1)} %maximum_select_fusion.1), channel_id=1, source_target_pairs={{0,7},{1,0},{2,1},{3,2},{4,3},{5,4},{6,5},{7,6},{8,15},{9,8},{10,9... | collective-permute-start | bytes 1179656 | tf_op jit(solution)/shard_map/ppermute | solution.py:30
  42.9 9.7 %collective-permute-start.2 = (bf16[384,2,256]{2,0,1:T(8,128)(2,1)S(1)}, bf16[384,2,256]{2,0,1:T(8,128)(2,1)S(1)}, u32[]{:S(2)}, u32[]{:S(2)}) collective-permute-start(bf16[384,2,256]{2,0,1:T(8,128)(2,1)S(1)} %collective-permute-done.1), channel_id=1, source_target_pairs={{0,1},{1,2},{2,3},{3,4},{4,5},{5,6},{6,7},{7,0},{8,9},{9,10},{10,1... | collective-permute-start | bytes 1179656 | tf_op jit(solution)/shard_map/ppermute | solution.py:27
  42.9 11.2 %collective-permute-start.6 = (bf16[384,2,256]{2,0,1:T(8,128)(2,1)S(1)}, bf16[384,2,256]{2,0,1:T(8,128)(2,1)S(1)}, u32[]{:S(2)}, u32[]{:S(2)}) collective-permute-start(bf16[384,2,256]{2,0,1:T(8,128)(2,1)S(1)} %collective-permute-done.5), channel_id=1, source_target_pairs={{0,7},{1,0},{2,1},{3,2},{4,3},{5,4},{6,5},{7,6},{8,15},{9,8},{10,9... | collective-permute-start | bytes 1179656 | tf_op jit(solution)/shard_map/ppermute | solution.py:30
  52.6 8.8 %collective-permute-start.3 = (bf16[384,2,256]{2,0,1:T(8,128)(2,1)S(1)}, bf16[384,2,256]{2,0,1:T(8,128)(2,1)S(1)}, u32[]{:S(2)}, u32[]{:S(2)}) collective-permute-start(bf16[384,2,256]{2,0,1:T(8,128)(2,1)S(1)} %collective-permute-done.2), channel_id=1, source_target_pairs={{0,1},{1,2},{2,3},{3,4},{4,5},{5,6},{6,7},{7,0},{8,9},{9,10},{10,1... | collective-permute-start | bytes 1179656 | tf_op jit(solution)/shard_map/ppermute | solution.py:27
  54.2 15.8 %collective-permute-start.7 = (bf16[384,2,256]{2,0,1:T(8,128)(2,1)S(1)}, bf16[384,2,256]{2,0,1:T(8,128)(2,1)S(1)}, u32[]{:S(2)}, u32[]{:S(2)}) collective-permute-start(bf16[384,2,256]{2,0,1:T(8,128)(2,1)S(1)} %collective-permute-done.6), channel_id=1, source_target_pairs={{0,7},{1,0},{2,1},{3,2},{4,3},{5,4},{6,5},{7,6},{8,15},{9,8},{10,9... | collective-permute-start | bytes 1179656 | tf_op jit(solution)/shard_map/ppermute | solution.py:30
  61.4 7.8 %collective-permute-start.4 = (bf16[384,2,256]{2,0,1:T(8,128)(2,1)S(1)}, bf16[384,2,256]{2,0,1:T(8,128)(2,1)S(1)}, u32[]{:S(2)}, u32[]{:S(2)}) collective-permute-start(bf16[384,2,256]{2,0,1:T(8,128)(2,1)S(1)} %collective-permute-done.3), channel_id=1, source_target_pairs={{0,1},{1,2},{2,3},{3,4},{4,5},{5,6},{6,7},{7,0},{8,9},{9,10},{10,1... | collective-permute-start | bytes 1179656 | tf_op jit(solution)/shard_map/ppermute | solution.py:27
  80.4 10.6 %collective-permute-start.8 = (bf16[384,4096]{0,1:T(8,128)(2,1)S(1)}, bf16[384,4096]{0,1:T(8,128)(2,1)}, u32[]{:S(2)}, u32[]{:S(2)}) collective-permute-start(bf16[384,4096]{0,1:T(8,128)(2,1)S(1)} %bitcast.97), channel_id=1, source_target_pairs={{0,16},{16,0},{32,48},{48,32},{64,80},{80,64},{96,112},{112,96},{1... | collective-permute-start | bytes 9437192 | tf_op jit(solution)/shard_map/ppermute | solution.py:94
  85.6 23.5 %collective-permute-start.10 = (bf16[448,4096]{1,0:T(8,128)(2,1)}, bf16[448,4096]{1,0:T(8,128)(2,1)}, u32[]{:S(2)}, u32[]{:S(2)}) collective-permute-start(bf16[448,4096]{1,0:T(8,128)(2,1)} %param.13), channel_id=1, source_target_pairs={{0,16},{16,0},{32,48},{48,32},{64,80},{80,64},{96,112},{112,96},{1... | collective-permute-start | bytes 11010056 | tf_op jit(solution)/shard_map/ppermute | solution.py:93
  85.9 5.1 %copy-start.4 = (bf16[4096,448]{0,1:T(8,128)(2,1)S(1)}, bf16[4096,448]{0,1:T(8,128)(2,1)}, u32[]{:S(2)}) copy-start(bf16[4096,448]{0,1:T(8,128)(2,1)} %param.11) | copy-start | bytes 11010052
  91.0 4.2 %copy-start.5 = (bf16[4096,448]{0,1:T(8,128)(2,1)S(1)}, bf16[4096,448]{0,1:T(8,128)(2,1)}, u32[]{:S(2)}) copy-start(bf16[4096,448]{0,1:T(8,128)(2,1)} %param.12) | copy-start | bytes 11010052
  99.8 9.3 %collective-permute-start.9 = (bf16[384,448]{0,1:T(8,128)(2,1)}, bf16[384,448]{0,1:T(8,128)(2,1)S(1)}, u32[]{:S(2)}, u32[]{:S(2)}) collective-permute-start(bf16[384,448]{0,1:T(8,128)(2,1)} %multiply_convert_fusion), channel_id=1, source_target_pairs={{0,16},{16,0},{32,48},{48,32},{64,80},{80,64},{96,112},{112,96},{1... | collective-permute-start | bytes 1032200 | tf_op jit(solution)/shard_map/ppermute | solution.py:103
  116.5 7.9 %collective-permute-start.11 = (bf16[192,2,256]{2,0,1:T(8,128)(2,1)S(1)}, bf16[192,2,256]{2,0,1:T(8,128)(2,1)}, u32[]{:S(2)}, u32[]{:S(2)}) collective-permute-start(bf16[192,2,256]{2,0,1:T(8,128)(2,1)S(1)} %select_bitcast_fusion.2), channel_id=1, source_target_pairs={{0,1},{1,2},{2,3},{3,4},{4,5},{5,6},{6,7},{7,0},{8,9},{9,10},{10,1... | collective-permute-start | bytes 589832 | tf_op jit(solution)/shard_map/ppermute | solution.py:52
  117.2 8.3 %collective-permute-start.18 = (bf16[192,2,256]{2,0,1:T(8,128)(2,1)S(1)}, bf16[192,2,256]{2,0,1:T(8,128)(2,1)S(1)}, u32[]{:S(2)}, u32[]{:S(2)}) collective-permute-start(bf16[192,2,256]{2,0,1:T(8,128)(2,1)S(1)} %select_bitcast_fusion.1), channel_id=1, source_target_pairs={{0,7},{1,0},{2,1},{3,2},{4,3},{5,4},{6,5},{7,6},{8,15},{9,8},{10,9... | collective-permute-start | bytes 589832 | tf_op jit(solution)/shard_map/ppermute | solution.py:53
  125.4 6.8 %collective-permute-start.12 = (bf16[192,2,256]{2,0,1:T(8,128)(2,1)S(1)}, bf16[192,2,256]{2,0,1:T(8,128)(2,1)S(1)}, u32[]{:S(2)}, u32[]{:S(2)}) collective-permute-start(bf16[192,2,256]{2,0,1:T(8,128)(2,1)S(1)} %add_convert_fusion.12), channel_id=1, source_target_pairs={{0,1},{1,2},{2,3},{3,4},{4,5},{5,6},{6,7},{7,0},{8,9},{9,10},{10,1... | collective-permute-start | bytes 589832 | tf_op jit(solution)/shard_map/ppermute | solution.py:52
  125.6 6.7 %collective-permute-start.19 = (bf16[192,2,256]{2,0,1:T(8,128)(2,1)S(1)}, bf16[192,2,256]{2,0,1:T(8,128)(2,1)S(1)}, u32[]{:S(2)}, u32[]{:S(2)}) collective-permute-start(bf16[192,2,256]{2,0,1:T(8,128)(2,1)S(1)} %add_convert_fusion.6), channel_id=1, source_target_pairs={{0,7},{1,0},{2,1},{3,2},{4,3},{5,4},{6,5},{7,6},{8,15},{9,8},{10,9... | collective-permute-start | bytes 589832 | tf_op jit(solution)/shard_map/ppermute | solution.py:53
  132.2 5.8 %collective-permute-start.13 = (bf16[192,2,256]{2,0,1:T(8,128)(2,1)S(1)}, bf16[192,2,256]{2,0,1:T(8,128)(2,1)S(1)}, u32[]{:S(2)}, u32[]{:S(2)}) collective-permute-start(bf16[192,2,256]{2,0,1:T(8,128)(2,1)S(1)} %add_convert_fusion.11), channel_id=1, source_target_pairs={{0,1},{1,2},{2,3},{3,4},{4,5},{5,6},{6,7},{7,0},{8,9},{9,10},{10,1... | collective-permute-start | bytes 589832 | tf_op jit(solution)/shard_map/ppermute | solution.py:52
  132.4 5.8 %collective-permute-start.20 = (bf16[192,2,256]{2,0,1:T(8,128)(2,1)S(1)}, bf16[192,2,256]{2,0,1:T(8,128)(2,1)S(1)}, u32[]{:S(2)}, u32[]{:S(2)}) collective-permute-start(bf16[192,2,256]{2,0,1:T(8,128)(2,1)S(1)} %add_convert_fusion.5), channel_id=1, source_target_pairs={{0,7},{1,0},{2,1},{3,2},{4,3},{5,4},{6,5},{7,6},{8,15},{9,8},{10,9... | collective-permute-start | bytes 589832 | tf_op jit(solution)/shard_map/ppermute | solution.py:53
  138.1 5.8 %collective-permute-start.14 = (bf16[192,2,256]{2,0,1:T(8,128)(2,1)S(1)}, bf16[192,2,256]{2,0,1:T(8,128)(2,1)S(1)}, u32[]{:S(2)}, u32[]{:S(2)}) collective-permute-start(bf16[192,2,256]{2,0,1:T(8,128)(2,1)S(1)} %add_convert_fusion.10), channel_id=1, source_target_pairs={{0,1},{1,2},{2,3},{3,4},{4,5},{5,6},{6,7},{7,0},{8,9},{9,10},{10,1... | collective-permute-start | bytes 589832 | tf_op jit(solution)/shard_map/ppermute | solution.py:52
  138.3 26.8 %copy-start.3 = (s32[128,2]{0,1:T(2,128)S(1)}, s32[128,2]{0,1:T(2,128)}, u32[]{:S(2)}) copy-start(s32[128,2]{0,1:T(2,128)} %param.10) | copy-start | bytes 3076
  138.3 5.8 %collective-permute-start.21 = (bf16[192,2,256]{2,0,1:T(8,128)(2,1)S(1)}, bf16[192,2,256]{2,0,1:T(8,128)(2,1)S(1)}, u32[]{:S(2)}, u32[]{:S(2)}) collective-permute-start(bf16[192,2,256]{2,0,1:T(8,128)(2,1)S(1)} %add_convert_fusion.4), channel_id=1, source_target_pairs={{0,7},{1,0},{2,1},{3,2},{4,3},{5,4},{6,5},{7,6},{8,15},{9,8},{10,9... | collective-permute-start | bytes 589832 | tf_op jit(solution)/shard_map/ppermute | solution.py:53
  144.0 5.8 %collective-permute-start.15 = (bf16[192,2,256]{2,0,1:T(8,128)(2,1)S(1)}, bf16[192,2,256]{2,0,1:T(8,128)(2,1)S(1)}, u32[]{:S(2)}, u32[]{:S(2)}) collective-permute-start(bf16[192,2,256]{2,0,1:T(8,128)(2,1)S(1)} %add_convert_fusion.9), channel_id=1, source_target_pairs={{0,1},{1,2},{2,3},{3,4},{4,5},{5,6},{6,7},{7,0},{8,9},{9,10},{10,1... | collective-permute-start | bytes 589832 | tf_op jit(solution)/shard_map/ppermute | solution.py:52
  144.2 40.4 %copy-start.2 = (s32[256,1]{0,1:T(1,128)S(1)}, s32[256,1]{0,1:T(1,128)}, u32[]{:S(2)}) copy-start(s32[256,1]{0,1:T(1,128)} %copy-done.1) | copy-start | bytes 3076
  144.2 5.8 %collective-permute-start.22 = (bf16[192,2,256]{2,0,1:T(8,128)(2,1)S(1)}, bf16[192,2,256]{2,0,1:T(8,128)(2,1)S(1)}, u32[]{:S(2)}, u32[]{:S(2)}) collective-permute-start(bf16[192,2,256]{2,0,1:T(8,128)(2,1)S(1)} %add_convert_fusion.3), channel_id=1, source_target_pairs={{0,7},{1,0},{2,1},{3,2},{4,3},{5,4},{6,5},{7,6},{8,15},{9,8},{10,9... | collective-permute-start | bytes 589832 | tf_op jit(solution)/shard_map/ppermute | solution.py:53
  149.9 6.6 %collective-permute-start.16 = (bf16[192,2,256]{2,0,1:T(8,128)(2,1)S(1)}, bf16[192,2,256]{2,0,1:T(8,128)(2,1)S(1)}, u32[]{:S(2)}, u32[]{:S(2)}) collective-permute-start(bf16[192,2,256]{2,0,1:T(8,128)(2,1)S(1)} %add_convert_fusion.8), channel_id=1, source_target_pairs={{0,1},{1,2},{2,3},{3,4},{4,5},{5,6},{6,7},{7,0},{8,9},{9,10},{10,1... | collective-permute-start | bytes 589832 | tf_op jit(solution)/shard_map/ppermute | solution.py:52
  150.0 6.6 %collective-permute-start.23 = (bf16[192,2,256]{2,0,1:T(8,128)(2,1)S(1)}, bf16[192,2,256]{2,0,1:T(8,128)(2,1)S(1)}, u32[]{:S(2)}, u32[]{:S(2)}) collective-permute-start(bf16[192,2,256]{2,0,1:T(8,128)(2,1)S(1)} %add_convert_fusion.2), channel_id=1, source_target_pairs={{0,7},{1,0},{2,1},{3,2},{4,3},{5,4},{6,5},{7,6},{8,15},{9,8},{10,9... | collective-permute-start | bytes 589832 | tf_op jit(solution)/shard_map/ppermute | solution.py:53
  156.6 8.0 %collective-permute-start.17 = (bf16[192,2,256]{2,0,1:T(8,128)(2,1)S(1)}, bf16[192,2,256]{2,0,1:T(8,128)(2,1)S(1)}, u32[]{:S(2)}, u32[]{:S(2)}) collective-permute-start(bf16[192,2,256]{2,0,1:T(8,128)(2,1)S(1)} %add_convert_fusion.7), channel_id=1, source_target_pairs={{0,1},{1,2},{2,3},{3,4},{4,5},{5,6},{6,7},{7,0},{8,9},{9,10},{10,1... | collective-permute-start | bytes 589832 | tf_op jit(solution)/shard_map/ppermute | solution.py:52
  156.7 7.8 %collective-permute-start.24 = (bf16[192,2,256]{2,0,1:T(8,128)(2,1)S(1)}, bf16[192,2,256]{2,0,1:T(8,128)(2,1)S(1)}, u32[]{:S(2)}, u32[]{:S(2)}) collective-permute-start(bf16[192,2,256]{2,0,1:T(8,128)(2,1)S(1)} %add_convert_fusion.1), channel_id=1, source_target_pairs={{0,7},{1,0},{2,1},{3,2},{4,3},{5,4},{6,5},{7,6},{8,15},{9,8},{10,9... | collective-permute-start | bytes 589832 | tf_op jit(solution)/shard_map/ppermute | solution.py:53
  164.7 4.9 %collective-permute-start.25 = (bf16[384,256]{1,0:T(8,128)(2,1)S(1)}, bf16[384,256]{1,0:T(8,128)(2,1)S(1)}, u32[]{:S(2)}, u32[]{:S(2)}) collective-permute-start(bf16[384,256]{1,0:T(8,128)(2,1)S(1)} %fusion.5), channel_id=1, source_target_pairs={{0,8},{1,9},{2,10},{3,11},{4,12},{5,13},{6,14},{7,15},{8,0},{9,1},... | collective-permute-start | bytes 589832 | tf_op jit(solution)/shard_map/ppermute | solution.py:59
  170.4 22.2 %all-to-all-start.1 = ((bf16[16,24,256]{2,1,0:T(8,128)(2,1)}), bf16[16,24,256]{2,1,0:T(8,128)(2,1)S(1)}, u32[]{:S(2)}, u32[]{:S(2)}) async-start(bf16[16,24,256]{2,1,0:T(8,128)(2,1)} %bitcast.39), calls=%async_computation.1 | async-start | bytes 393216 | tf_op jit(solution)/shard_map/all_to_all | solution.py:107
  (1 other events, 0.6 us)
